TPU v7x, 128 devices: a whole 4x4x4 slice. The times are simulated.
128 devices in a mesh: gx: 8 (over x, core), gy: 4 (over z), gz: 4 (over y).
Axes of the slice: x: 4, y: 4, z: 4, core: 2. Of those that a mesh axis runs over, the one named last changes fastest.
Arguments:
- velocity: float32 [3, 256, 256, 512], P(None, 'gx', 'gy', 'gz'), may hold values from -12 to 12
- inv_density: float32 [256, 256, 512], P('gx', 'gy', 'gz'), may hold values from 0.2 to 5
- factor_x: float32 [256, 64], P('gx'), may hold values from -0.5 to 0.5
- factor_y: float32 [256, 64], P('gy'), may hold values from -0.5 to 0.5
- factor_z: float32 [512, 64], P('gz'), may hold values from -0.375 to 0.375
Outputs:
- pressure: float32 [256, 256, 512], P('gx', 'gy', 'gz')
- corrected: float32 [3, 256, 256, 512], P(None, 'gx', 'gy', 'gz')
- core: float32 [64, 4, 64, 64], P('gx', None, 'gy', 'gz')
All inputs are finite; a program needn't handle non-finite values.
Results may differ from a plain program's by a relative error of at most 0.00013.
Values sent between devices are 32-bit elements; how exact they have to be, the bound alone decides.
A program may use at most 128 MiB of HBM per device.

v0:
```python
import jax
import jax.numpy as jnp
from jax import lax
from jax.sharding import PartitionSpec as P

ITERS = 4


SHIFT = 0.1
HIGHEST = lax.Precision.HIGHEST


def padded_2(cells, sides, width):
    for axis, dim in sides:
        count = lax.axis_size(axis)
        ends = count - 1
        head = lax.slice_in_dim(cells, 0, width, axis=dim)
        tail = lax.slice_in_dim(cells, cells.shape[dim] - width, cells.shape[dim], axis=dim)
        cells = jnp.concatenate(
            [
                lax.ppermute(tail, axis, [(i, (i + 1) % count) for i in range(ends)]),
                cells,
                lax.ppermute(head, axis, [((i + 1) % count, i) for i in range(ends)]),
            ],
            axis=dim,
        )
    return cells


def neighbours(padded):
    centre_cut = (slice(None),) + (slice(1, -1),) * 3
    result = []
    for dimension in range(1, 4):
        forward = list(centre_cut)
        forward[dimension] = slice(2, None)
        backward = list(centre_cut)
        backward[dimension] = slice(None, -2)
        result.append((padded[tuple(forward)], padded[tuple(backward)]))
    return result


def widen(stack):
    return padded_2(stack, (("gx", 1), ("gy", 2), ("gz", 3)), 1)


def assemble(sides, inv_density):
    couplings = []
    diagonal = SHIFT + jnp.zeros_like(inv_density)
    divergence = jnp.zeros_like(inv_density)
    for dimension in range(3):
        forward, backward = sides[dimension]
        c_forward = 0.5 * (inv_density + forward[3])
        c_backward = 0.5 * (inv_density + backward[3])
        couplings.append((c_forward, c_backward))
        diagonal = diagonal + c_forward + c_backward
        divergence = divergence + 0.5 * (forward[dimension] - backward[dimension])
    return (couplings, diagonal, -divergence)


def apply_operator(sides, field, couplings, diagonal):
    result = diagonal * field
    for dimension in range(3):
        forward, backward = sides[dimension]
        result = (
            result - couplings[dimension][0] * forward[0] - couplings[dimension][1] * backward[0]
        )
    return result


def correct(sides, velocity, inv_density):
    parts = []
    for dimension in range(3):
        gradient = 0.5 * (sides[dimension][0][0] - sides[dimension][1][0])
        parts.append(velocity[dimension] - inv_density * gradient)
    return jnp.stack(parts, 0)


def residual_product(residual, precond):
    return lax.psum(jnp.sum(residual * precond), ("gx", "gy", "gz"))


def per_device(velocity, inv_density, factor_x, factor_y, factor_z):
    padded = widen(jnp.concatenate([velocity, inv_density[None]], 0))
    couplings, diagonal, rhs = assemble(neighbours(padded), inv_density)
    pressure = jnp.zeros_like(rhs)
    residual = rhs
    precond = residual / diagonal
    direction = precond
    product = residual_product(residual, precond)
    for iteration in range(ITERS):
        image = apply_operator(neighbours(widen(direction[None])), direction, couplings, diagonal)
        alpha = product / lax.psum(jnp.sum(direction * image), ("gx", "gy", "gz"))
        pressure = pressure + alpha * direction
        residual = residual - alpha * image
        precond = residual / diagonal
        fresh = residual_product(residual, precond)
        direction = precond + fresh / product * direction
        product = fresh
    corrected = correct(neighbours(widen(pressure[None])), velocity, inv_density)
    fields = jnp.concatenate([corrected, pressure[None]], 0)
    cells_x, cells_y = (fields.shape[1], fields.shape[2])
    rank = factor_x.shape[1]
    groups_x = lax.axis_size("gx")
    groups_y = lax.axis_size("gy")
    groups_z = lax.axis_size("gz")
    split_x = factor_x.reshape(cells_x, groups_x, rank // groups_x)
    split_y = factor_y.reshape(cells_y, groups_y, rank // groups_y)
    split_z = factor_z.reshape(factor_z.shape[0], groups_z, rank // groups_z)
    first = jnp.einsum("fijk,iPa->Pafjk", fields, split_x, precision=HIGHEST)
    second = jnp.einsum("Pafjk,jQb->PQafbk", first, split_y, precision=HIGHEST)
    third = jnp.einsum("PQafbk,kRc->PQRafbc", second, split_z, precision=HIGHEST)
    flat = third.reshape(groups_x * groups_y * groups_z, -1)
    mine = lax.psum_scatter(flat, ("gx", "gy", "gz"), scatter_dimension=0, tiled=True)
    core = mine.reshape(rank // groups_x, 4, rank // groups_y, rank // groups_z)
    return (pressure, corrected, core)


def solution(mesh):
    placed = (
        P(None, "gx", "gy", "gz"),
        P("gx", "gy", "gz"),
        P("gx", None),
        P("gy", None),
        P("gz", None),
    )
    return jax.shard_map(
        per_device,
        mesh=mesh,
        in_specs=placed,
        out_specs=(P("gx", "gy", "gz"), P(None, "gx", "gy", "gz"), P("gx", None, "gy", "gz")),
        check_vma=False,
    )
```

profile of v0, /device:TPU:1, one launch (start us, length us, event | category | flops | bytes accessed | tf_op | source)
XLA Modules:
  0.0 1010.2 jit_solution(12540318608828455812)
XLA Ops:
  28.8 5.8 fusion.140
  34.6 5.8 copy.13
  41.7 5.8 copy.15
  52.2 5.1 copy.14
  62.4 12.2 %fusion.132 = (f32[32,64,128]{2,0,1:T(8,128)S(1)}, f32[32,64,128]{2,0,1:T(8,128)}, f32[32,64,128]{2,0,1:T(8,128)}, f32[32,64,128]{2,0,1:T(8,128)}, f32[32,64,128...) fusion(f32[4,1,64,128]{3,1,2,0:T(1,128)S(1)} %collective-permut, ...), kind=kLoop, calls=%fused_computation.296 | loop fusion | flops 19398656 | bytes 15153280 | tf_op jit(solution)/shard_map/div | solution.py:87
  76.5 5.9 collective-permute-start.7
  104.6 10.3 %multiply_reduce_fusion.5 = (f32[]{:T(128)}, f32[]{:T(128)}, f32[32,64,128]{2,0,1:T(8,128)}) fusion(f32[32,64,128]{2,0,1:T(8,128)} %copy-done.6, f32[32,64,128]{2,0,1:T(8,128)} %get-tuple-element.29, f32[32,64,128]{2,0,1:T(8,128)} %get-tuple-element.28, f32[1,34,1,128]{3,1,2,0:T(8,128)S(1)} %collective-permute-done.8, ...), kind=kLoop, calls=%fused_computation.267 | loop fusion | flops 9175038 | bytes 11652648 | tf_op jit(solution)/shard_map/reduce_sum | solution.py:92
  114.9 69.9 %all-reduce.1 = (f32[]{:T(128)}, f32[]{:T(128)}) all-reduce(f32[]{:T(128)} %get-tuple-element.7, f32[]{:T(128)} %get-tuple-element.6), channel_id=1, replica_groups=mesh['gx'=8,'gy'=4,'gz'=4] {'gx','gy','gz'}, use_global_device_ids=true, to_apply=%region_1.0 | all-reduce | flops 2 | bytes 16 | tf_op jit(solution)/shard_map/psum | solution.py:79
  190.3 64.4 %psum.58 = f32[]{:T(128)} all-reduce(f32[]{:T(128)} %get-tuple-element.17), channel_id=1, replica_groups=mesh['gx'=8,'gy'=4,'gz'=4] {'gx','gy','gz'}, use_global_device_ids=true, to_apply=%region_5.0 | all-reduce | flops 1 | bytes 8 | tf_op jit(solution)/shard_map/psum | solution.py:79
  284.9 10.0 multiply_reduce_fusion.3
  294.8 65.5 %psum.59 = f32[]{:T(128)} all-reduce(f32[]{:T(128)} %get-tuple-element.15), channel_id=1, replica_groups=mesh['gx'=8,'gy'=4,'gz'=4] {'gx','gy','gz'}, use_global_device_ids=true, to_apply=%region_7.0 | all-reduce | flops 1 | bytes 8 | tf_op jit(solution)/shard_map/psum | solution.py:92
  365.9 63.7 %psum.60 = f32[]{:T(128)} all-reduce(f32[]{:T(128)} %get-tuple-element.12), channel_id=1, replica_groups=mesh['gx'=8,'gy'=4,'gz'=4] {'gx','gy','gz'}, use_global_device_ids=true, to_apply=%region_9.0 | all-reduce | flops 1 | bytes 8 | tf_op jit(solution)/shard_map/psum | solution.py:79
  460.3 9.7 multiply_reduce_fusion.1
  469.9 65.6 %psum.61 = f32[]{:T(128)} all-reduce(f32[]{:T(128)} %get-tuple-element.10), channel_id=1, replica_groups=mesh['gx'=8,'gy'=4,'gz'=4] {'gx','gy','gz'}, use_global_device_ids=true, to_apply=%region_11.0 | all-reduce | flops 1 | bytes 8 | tf_op jit(solution)/shard_map/psum | solution.py:92
  539.7 63.3 %psum.62 = f32[]{:T(128)} all-reduce(f32[]{:T(128)} %multiply_reduce_fusion), channel_id=1, replica_groups=mesh['gx'=8,'gy'=4,'gz'=4] {'gx','gy','gz'}, use_global_device_ids=true, to_apply=%region_13.0 | all-reduce | flops 1 | bytes 8 | tf_op jit(solution)/shard_map/psum | solution.py:79
  634.2 9.1 fusion.33
  643.3 65.6 %psum.63 = f32[]{:T(128)} all-reduce(f32[]{:T(128)} %fusion.33), channel_id=1, replica_groups=mesh['gx'=8,'gy'=4,'gz'=4] {'gx','gy','gz'}, use_global_device_ids=true, to_apply=%region_15.0 | all-reduce | flops 1 | bytes 8 | tf_op jit(solution)/shard_map/psum | solution.py:92
  739.0 5.3 fusion.28
  751.6 7.1 fusion.10
  758.7 17.2 %fusion.1 = f32[8,8,4,128,4,16]{3,5,2,1,4,0:T(8,128)} fusion(f32[64,4,16,1,1,1]{0,2,5,4,1,3:T(8,128)S(1)} %bitcast.369, f32[8,8,4,64,128,1]{4,1,0,3,2,5:T(8,128)S(1)} %fusion.10), kind=kOutput, calls=%fused_computation.2 | convolution fusion | flops 1610612736 | bytes 16793600 | tf_op jit(solution)/shard_map/Pafjk,jQb->PQafbk/dot_general | solution.py:110
  775.9 28.8 %convolution_bitcast_fusion = f32[8,4,4,8,4,16,16]{6,5,2,4,3,1,0:T(8,128)S(1)} fusion(f32[128,4,16,1,1,1,1]{0,2,1,6,5,4,3:T(8,128)S(1)} %bitcast.342, f32[8,8,4,128,4,16]{3,5,2,1,4,0:T(8,128)} %fusion.1), kind=kOutput, calls=%fused_computation | convolution fusion | flops 1610612736 | bytes 12615680 | tf_op jit(solution)/shard_map/PQafbk,kRc->PQRafbc/dot_general | solution.py:111
  804.7 12.7 %copy.52 = f32[8,4,4,8,4,16,16]{6,5,4,3,2,1,0:T(8,128)} copy(f32[8,4,4,8,4,16,16]{6,5,2,4,3,1,0:T(8,128)S(1)} %convolution_bitcast_fusion) | data formatting | bytes 8388608 | tf_op jit(solution)/shard_map/PQafbk,kRc->PQRafbc/transpose | solution.py:111
  817.5 28.3 %reshape.40 = f32[128,8192]{1,0:T(8,128)} reshape(f32[8,4,4,8,4,16,16]{6,5,4,3,2,1,0:T(8,128)} %copy.52) | data formatting | bytes 8388608 | tf_op jit(solution)/shard_map/reshape | solution.py:112
  853.6 147.4 %all-reduce.4.cloned.1.call-done = f32[128,8192]{1,0:T(8,128)} async-done(((f32[128,8192]{1,0:T(8,128)}), f32[128,8192]{1,0:T(8,128)}) %all-reduce.4.cloned.1.call-update) | async-done | bytes 4194320
  (170 shorter events, 201.4 us)
Async XLA Ops:
  7.2 993.8 %all-reduce.4.cloned.1.call-start = ((), (), s32[]{:S(2)}) async-start(), calls=%async_computation | async-start | bytes 8388608
  11.9 7.1 collective-permute-start
  21.6 5.6 collective-permute-start.3
  40.4 11.8 %collective-permute-start.4 = (f32[4,34,66,1]{2,0,3,1:T(4,128)}, f32[4,34,66,1]{2,0,3,1:T(4,128)}, u32[]{:S(2)}, u32[]{:S(2)}) collective-permute-start(f32[4,34,66,1]{2,0,3,1:T(4,128)} %copy.13), channel_id=1, source_target_pairs={{1,0},{2,1},{3,2},{5,4},{6,5},{7,6},{9,8},{10,9},{11,10},{13,12},{... | collective-permute-start | bytes 107720 | tf_op jit(solution)/shard_map/ppermute | solution.py:23
  47.5 9.9 collective-permute-start.5
  74.6 7.8 collective-permute-start.6
  76.5 6.9 collective-permute-start.7
  83.4 5.9 collective-permute-start.8
  84.7 5.5 collective-permute-start.9
  94.2 7.1 collective-permute-start.10
  97.3 5.7 collective-permute-start.11
  257.7 5.6 collective-permute-start.12
  274.5 7.1 collective-permute-start.16
  277.5 5.7 collective-permute-start.17
  432.7 5.6 collective-permute-start.18
  449.4 7.5 collective-permute-start.22
  452.5 6.1 collective-permute-start.23
  607.0 5.6 collective-permute-start.24
  623.8 7.1 collective-permute-start.28
  626.9 5.7 collective-permute-start.29
  713.0 6.4 collective-permute-start.30
  720.4 5.6 collective-permute-start.32
  731.8 12.5 %collective-permute-start.34 = (f32[1,34,66,1]{2,1,3,0:T(8,128)S(1)}, f32[1,34,66,1]{2,1,3,0:T(8,128)S(1)}, u32[]{:S(2)}, u32[]{:S(2)}) collective-permute-start(f32[1,34,66,1]{2,1,3,0:T(8,128)S(1)} %copy.44), channel_id=1, source_target_pairs={{1,0},{2,1},{3,2},{5,4},{6,5},{7,6},{9,8},{10,9},{11,10},{13,12},{... | collective-permute-start | bytes 26936 | tf_op jit(solution)/shard_map/ppermute | solution.py:23
  735.0 11.0 %collective-permute-start.35 = (f32[1,34,66,1]{2,1,3,0:T(8,128)S(1)}, f32[1,34,66,1]{2,1,3,0:T(8,128)S(1)}, u32[]{:S(2)}, u32[]{:S(2)}) collective-permute-start(f32[1,34,66,1]{2,1,3,0:T(8,128)S(1)} %copy.46), channel_id=1, source_target_pairs={{0,1},{1,2},{2,3},{4,5},{5,6},{6,7},{8,9},{9,10},{10,11},{12,13},{... | collective-permute-start | bytes 26936 | tf_op jit(solution)/shard_map/ppermute | solution.py:21
  (31 other events, 968.0 us)
Sparse Core Ops, SparseCore 0:
  845.9 155.0 all-reduce.3
where the time goes:
time: 1020 us; the launch traced here: 1010 us
  blocking collectives  458 us (45%)
  waiting for transfers between devices  160 us (16%)
  local copies, waits for them, and re-layouts  126 us (12%)
  starting transfers between devices  103 us (10%)
  other arithmetic  86 us (8%)
  matrix products  53.1 us (5%)
  between operations  24.4 us (2%)
    psum x4, blocking collectives, residual_product(): return lax.psum(jnp.sum(residual * precond), ('gx', 'gy', 'gz'))  261 us
    psum x3, blocking collectives, per_device(): alpha = product / lax.psum(jnp.sum(direction * image), ('gx', 'gy', 'gz'))  197 us
    unnamed x2, waiting for transfers between devices  147 us
    ppermute x18, starting transfers between devices, padded_2(): lax.ppermute(tail, axis, [(i, (i + 1) % count) for i in range(ends)])  70.9 us
    reduce_sum x4, other arithmetic, per_device(): alpha = product / lax.psum(jnp.sum(direction * image), ('gx', 'gy', 'gz'))  39 us
    ppermute x18, starting transfers between devices, padded_2(): lax.ppermute(head, axis, [((i + 1) % count, i) for i in range(ends)])  32 us
    dot_general x1, matrix products, per_device(): jnp.einsum('PQafbk,kRc->PQRafbc', second, split_z, precision=HIGHEST)  28.8 us
    reshape x1, local copies, waits for them, and re-layouts, per_device(): flat = third.reshape(groups_x * groups_y * groups_z, -1)  28.3 us
  transfers between devices with their start and end apart: 37, of which 14 were waited for; matrix products, arithmetic and copies ran while one was open for 4% of the time, Pallas kernels for 0%

commit v1 on v0

v1 whole, which is shorter than its diff:
```python
import jax
import jax.numpy as jnp
from jax import lax
from jax.experimental import pallas as pl
from jax.experimental.pallas import tpu as pltpu
from jax.sharding import PartitionSpec as P

ITERS = 4
SHIFT = 0.1
MESH = pl.DeviceIdType.MESH
F32 = jnp.float32
BF16 = jnp.bfloat16
NI, NJ, NK = 32, 64, 128
TOP = 8
AXES = ("gx", "gy", "gz")
SIZES = (8, 4, 4)
PLANE = [(dy, dz) for dy in range(4) for dz in range(4) if dy or dz]
ROUTES = {3: ("gz", 1), 1: ("gy", 1), 0: ("gz", -1), 2: ("gy", -1)}
ORDER = (3, 1, 0, 2)
TINY = 1e-11


def two_sum(a, b):
    s = a + b
    t = s - a
    return s, (a - (s - t)) + (b - t)


def quick(a, b):
    s = a + b
    return s, b - (s - a)


def df_add(x, y):
    s, e = two_sum(x[0], y[0])
    return quick(s, e + (x[1] + y[1]))


def df_neg(x):
    return -x[0], -x[1]


def halves(a):
    t = 4097.0 * a
    h = t - (t - a)
    return h, a - h


def df_mul(x, y):
    p = x[0] * y[0]
    ah, al = halves(x[0])
    bh, bl = halves(y[0])
    e = ((ah * bh - p) + ah * bl + al * bh) + al * bl
    return quick(p, e + (x[0] * y[1] + x[1] * y[0]))


def df_recip(x):
    r = 1.0 / x[0]
    one = (jnp.ones_like(r), jnp.zeros_like(r))
    two = (jnp.full_like(r, 2.0), jnp.zeros_like(r))
    y = (r, jnp.zeros_like(r))
    for _ in range(2):
        y = df_mul(y, df_add(two, df_neg(df_mul(x, y))))
    return y


def solve4(nu):
    n = ITERS
    g = [[None] * n for _ in range(n)]
    for i in range(n):
        for j in range(i + 1):
            g[i][j] = df_add(nu[i + j], df_neg(nu[i + j + 1]))
    y = list(nu[:n])
    low = [[None] * n for _ in range(n)]
    inv = []
    for k in range(n):
        pivot = g[k][k]
        start = nu[2 * k][0] - nu[2 * k + 1][0]
        ok = pivot[0] > TINY * start
        safe = (jnp.where(ok, pivot[0], 1.0), jnp.where(ok, pivot[1], 0.0))
        r = df_recip(safe)
        r = (jnp.where(ok, r[0], 0.0), jnp.where(ok, r[1], 0.0))
        inv.append(r)
        for i in range(k + 1, n):
            low[i][k] = df_mul(g[i][k], r)
        for i in range(k + 1, n):
            for j in range(k + 1, i + 1):
                g[i][j] = df_add(g[i][j], df_neg(df_mul(low[i][k], g[j][k])))
            y[i] = df_add(y[i], df_neg(df_mul(low[i][k], y[k])))
    c = [None] * n
    for i in reversed(range(n)):
        v = df_mul(y[i], inv[i])
        for j in range(i + 1, n):
            v = df_add(v, df_neg(df_mul(low[j][i], c[j])))
        c[i] = v
    return [v[0] for v in c]


def lanes(shape):
    return lax.broadcasted_iota(jnp.int32, shape, len(shape) - 1)


def rows(shape):
    return lax.broadcasted_iota(jnp.int32, shape, 0)


def split(x):
    hi = x.astype(BF16)
    return hi, (x - hi.astype(F32)).astype(BF16)


def dot(a, b):
    return lax.dot_general(a, b, (((1,), (0,)), ((), ())), preferred_element_type=F32)


def squeeze_face(face):
    lane = lanes((8, 128))
    halves_ = []
    for h in range(2):
        acc = face[32 * h : 32 * h + 8]
        for q in range(1, 4):
            part = face[32 * h + 8 * q : 32 * h + 8 * q + 8]
            acc = jnp.where(lane // 32 == q, pltpu.roll(part, 32 * q, 1), acc)
        halves_.append(acc)
    return jnp.concatenate(halves_, axis=0)


def spread_face(packed):
    parts = []
    for h in range(2):
        for q in range(4):
            part = packed[8 * h : 8 * h + 8]
            parts.append(part if q == 0 else pltpu.roll(part, 128 - 32 * q, 1))
    return jnp.concatenate(parts, axis=0)


def fold(x):
    t = [x[8 * q : 8 * q + 8] for q in range(8)]
    return ((t[0] + t[1]) + (t[2] + t[3])) + ((t[4] + t[5]) + (t[6] + t[7]))


def kernel(
    vel, inv, fx, fy, fz,
    out_p, out_c, out_core,
    vx, vy, vz, ip, w, cx, cy, cz, dinv, pp, pst, cst,
    ysend, yrecv, zsend, zrecv, ysend0, yrecv0, zsend0, zrecv0,
    a_send, a_recv0, a_recv1,
    wz_hi, wz_lo, fyt, k_hi, k_lo, xh, xl, u,
    za_in, za_acc, za_dir, za_out, ya_in, ya_acc, ya_dir, ya_out,
    b_src_z, b_src_y, b_in, b_acc, b_dir, b_out, ysc, v, v_recv,
    in_sem, out_sem, hs_sem, hr_sem, as_sem, ar_sem, rs_sem, rr_sem, xs_sem, xr_sem,
):
    me = [lax.axis_index(a) for a in AXES]
    has = []
    for a in range(3):
        has += [me[a] > 0, me[a] < SIZES[a] - 1]

    def neighbour(side):
        a = side // 2
        step = 1 if side % 2 else SIZES[a] - 1
        return {AXES[a]: lax.rem(me[a] + step, SIZES[a])}

    def remote(src, dst, ss, rs, dev):
        return pltpu.make_async_remote_copy(
            src_ref=src, dst_ref=dst, send_sem=ss, recv_sem=rs, device_id=dev, device_id_type=MESH
        )

    lane = lanes((NJ, NK))

    loads = [
        pltpu.make_async_copy(inv, ip.at[pl.ds(1, NI), pl.ds(TOP, NJ)], in_sem.at[0]),
        pltpu.make_async_copy(vel.at[2], vz, in_sem.at[1]),
        pltpu.make_async_copy(vel.at[1], vy.at[:, pl.ds(TOP, NJ)], in_sem.at[2]),
        pltpu.make_async_copy(vel.at[0], vx.at[pl.ds(1, NI)], in_sem.at[3]),
    ]
    for c in loads:
        c.start()

    barrier = pltpu.get_barrier_semaphore()
    for o in range(1, 8):
        pl.semaphore_signal(barrier, inc=1, device_id={"gx": lax.rem(me[0] + o, 8)}, device_id_type=MESH)
    for dy, dz in PLANE:
        pl.semaphore_signal(
            barrier, inc=1,
            device_id={"gy": lax.rem(me[1] + dy, 4), "gz": lax.rem(me[2] + dz, 4)},
            device_id_type=MESH,
        )

    zero_plane = jnp.zeros((NJ, NK), F32)
    for s in range(2):
        far = (0, NI + 1)[s]

        @pl.when(jnp.logical_not(has[s]))
        def _():
            vx[far] = zero_plane
            ip[far, pl.ds(TOP, NJ)] = zero_plane
            for k in range(ITERS):
                w[k, far, pl.ds(TOP, NJ)] = zero_plane

        @pl.when(jnp.logical_not(has[2 + s]))
        def _():
            yrecv0[s] = jnp.zeros((2, NI, NK), F32)
            for k in range(ITERS):
                yrecv[k, s] = jnp.zeros((NI, NK), F32)

        @pl.when(jnp.logical_not(has[4 + s]))
        def _():
            zrecv0[s] = jnp.zeros((2, 16, NK), F32)
            for k in range(ITERS):
                zrecv[k, s] = jnp.zeros((16, NK), F32)

    pl.semaphore_wait(barrier, 7 + len(PLANE))

    def halo(r, side, landing):
        near = (1, NI)[side % 2]
        far = (0, NI + 1)[landing % 2]
        s, t = side % 2, landing % 2
        ax = side // 2
        if r == 0:
            if ax == 0:
                edge = (0, NI - 1)[s]
                pairs = [
                    (vel.at[0, edge], vx.at[far]),
                    (inv.at[edge], ip.at[far, pl.ds(TOP, NJ)]),
                ]
            elif ax == 1:
                pairs = [(ysend0.at[s], yrecv0.at[t])]
            else:
                pairs = [(zsend0.at[s], zrecv0.at[t])]
        else:
            k = r - 1
            if ax == 0:
                pairs = [(w.at[k, near, pl.ds(TOP, NJ)], w.at[k, far, pl.ds(TOP, NJ)])]
            elif ax == 1:
                pairs = [(ysend.at[k, s], yrecv.at[k, t])]
            else:
                pairs = [(zsend.at[k, s], zrecv.at[k, t])]
        return [
            remote(a, b, hs_sem.at[r, side, n], hr_sem.at[r, landing, n], neighbour(side))
            for n, (a, b) in enumerate(pairs)
        ]

    def halo_start(r, sides):
        for side in sides:
            @pl.when(has[side])
            def _():
                for c in halo(r, side, side ^ 1):
                    c.start()

    def halo_wait(r, sides):
        for side in sides:
            @pl.when(has[side])
            def _():
                for c in halo(r, side, side):
                    c.wait_recv()

    def halo_sent(r, sides):
        for side in sides:
            @pl.when(has[side])
            def _():
                for c in halo(r, side, side ^ 1):
                    c.wait_send()

    halo_start(0, (0, 1))

    def take(acc, x, i, edge):
        moved = pltpu.roll(x, i if edge == 0 else i + 1, 1)
        return jnp.where(lane == i, moved, acc)

    for c in loads[:3]:
        c.wait()

    def face0(i, carry):
        u0, u1, n0, n1 = carry
        a = vz[i]
        b = ip[i + 1, pl.ds(TOP, NJ)]
        row = pl.ds(i, 1)
        ysend0[0, 0, row] = vy[i, pl.ds(TOP, 1)]
        ysend0[1, 0, row] = vy[i, pl.ds(TOP + NJ - 1, 1)]
        ysend0[0, 1, row] = b[0:1]
        ysend0[1, 1, row] = b[NJ - 1 : NJ]
        return take(u0, a, i, 0), take(u1, a, i, 1), take(n0, b, i, 0), take(n1, b, i, 1)

    u0, u1, n0, n1 = lax.fori_loop(0, NI, face0, (zero_plane,) * 4, unroll=2)
    zsend0[0, 0] = squeeze_face(u0)
    zsend0[1, 0] = squeeze_face(u1)
    zsend0[0, 1] = squeeze_face(n0)
    zsend0[1, 1] = squeeze_face(n1)
    halo_start(0, (2, 3, 4, 5))
    loads[3].wait()

    z64 = jnp.zeros((NK, 64), F32)
    fzp = jnp.concatenate([fz[...], z64], axis=1)
    lane_k = lanes((NK, 128))

    def build_z(i8, _):
        row = pl.ds(pl.multiple_of(i8 * 128, 128), 128)
        for r in range(4):
            moved = pltpu.roll(fzp, lax.rem(16 * i8 + 128 - 16 * r, 128), 1)
            hi, lo = split(jnp.where(lane_k // 16 == i8, moved, 0.0))
            wz_hi[row, pl.ds(128 * r, 128)] = hi
            wz_lo[row, pl.ds(128 * r, 128)] = lo
        return 0

    lax.fori_loop(0, 8, build_z, 0)
    fyp = jnp.concatenate([fy[...], jnp.zeros((NJ, 64), F32)], axis=1)
    hi, lo = split(fyp.T[:64])
    fyt[...] = jnp.concatenate([hi, lo, hi], axis=1)
    fx_hi, fx_lo = split(fx[...])
    rep = (rows((512, NI)) // 16 == lanes((512, NI))).astype(F32).astype(BF16)
    same = (rows((512, 128)) % 16) == (lanes((512, 128)) % 16)

    def build_x(m, _):
        pick = (rows((64, 128)) == 8 * m + lanes((64, 128)) // 16).astype(F32).astype(BF16)
        for part, dst in ((fx_hi, k_hi), (fx_lo, k_lo)):
            wide = dot(part, pick).astype(BF16)
            dst[m] = jnp.where(same, dot(rep, wide), 0.0).astype(BF16)
        return 0

    lax.fori_loop(0, 8, build_x, 0)

    halo_wait(0, range(6))

    def ahead(x, face, i):
        return pltpu.roll(jnp.where(lane == 0, pltpu.roll(face, lax.rem(NK - i, NK), 1), x), NK - 1, 1)

    def behind(x, face, i):
        return pltpu.roll(jnp.where(lane == NK - 1, pltpu.roll(face, NK - 1 - i, 1), x), 1, 1)

    um, up = spread_face(zrecv0[0, 0]), spread_face(zrecv0[1, 0])
    nm, np_ = spread_face(zrecv0[0, 1]), spread_face(zrecv0[1, 1])
    czb = 0.5 * (n0 + nm)
    zero_acc = jnp.zeros((8, NK), F32)

    def accumulate(acc, x):
        s, e = two_sum(acc[0], fold(x))
        return s, acc[1] + e

    def first(i, carry):
        z0, z1, acc = carry
        row = pl.ds(i, 1)
        ip[i + 1, pl.ds(TOP - 1, 1)] = yrecv0[0, 1, row]
        ip[i + 1, pl.ds(TOP + NJ, 1)] = yrecv0[1, 1, row]
        vy[i, pl.ds(TOP - 1, 1)] = yrecv0[0, 0, row]
        vy[i, pl.ds(TOP + NJ, 1)] = yrecv0[1, 0, row]
        n = ip[i + 1, pl.ds(TOP, NJ)]
        xb = 0.5 * (n + ip[i, pl.ds(TOP, NJ)])
        xf = 0.5 * (n + ip[i + 2, pl.ds(TOP, NJ)])
        yb = 0.5 * (n + ip[i + 1, pl.ds(TOP - 1, NJ)])
        yf = 0.5 * (n + ip[i + 1, pl.ds(TOP + 1, NJ)])
        zb = 0.5 * (n + behind(n, nm, i))
        zf = 0.5 * (n + ahead(n, np_, i))
        cx[i] = xb
        cx[i + 1] = xf
        cy[i, pl.ds(TOP, NJ)] = yf
        cy[i, pl.ds(TOP - 1, 1)] = yb[0:1]
        cz[i] = zf
        d = SHIFT + xf + xb + yf + yb + zf + zb
        a = vz[i]
        div = 0.5 * (vx[i + 2] - vx[i])
        div = div + 0.5 * (vy[i, pl.ds(TOP + 1, NJ)] - vy[i, pl.ds(TOP - 1, NJ)])
        div = div + 0.5 * (ahead(a, up, i) - behind(a, um, i))
        b = -div
        di = 1.0 / d
        dinv[i] = di
        w0 = b * di
        w[0, i + 1, pl.ds(TOP, NJ)] = w0
        ysend[0, 0, row] = w0[0:1]
        ysend[0, 1, row] = w0[NJ - 1 : NJ]
        return take(z0, w0, i, 0), take(z1, w0, i, 1), accumulate(acc, b * w0)

    z0, z1, acc = lax.fori_loop(0, NI, first, (zero_plane, zero_plane, (zero_acc, zero_acc)))
    moments = [acc]

    faces = []
    for k in range(ITERS):
        zsend[k, 0] = squeeze_face(z0)
        zsend[k, 1] = squeeze_face(z1)
        halo_start(k + 1, range(6))
        halo_wait(k + 1, range(6))
        wm, wp = spread_face(zrecv[k, 0]), spread_face(zrecv[k, 1])
        flux = czb * wm
        last = k == ITERS - 1

        def step(i, carry):
            z0, z1, odd, even = carry
            row = pl.ds(i, 1)
            w[k, i + 1, pl.ds(TOP - 1, 1)] = yrecv[k, 0, row]
            w[k, i + 1, pl.ds(TOP + NJ, 1)] = yrecv[k, 1, row]
            c = w[k, i + 1, pl.ds(TOP, NJ)]
            f = cz[i]
            bw = cx[i] * w[k, i, pl.ds(TOP, NJ)] + cx[i + 1] * w[k, i + 2, pl.ds(TOP, NJ)]
            bw = bw + cy[i, pl.ds(TOP - 1, NJ)] * w[k, i + 1, pl.ds(TOP - 1, NJ)]
            bw = bw + cy[i, pl.ds(TOP, NJ)] * w[k, i + 1, pl.ds(TOP + 1, NJ)]
            bw = bw + (f * ahead(c, wp, i) + behind(f * c, flux, i))
            odd = accumulate(odd, c * bw)
            if not last:
                nw = bw * dinv[i]
                even = accumulate(even, bw * nw)
                w[k + 1, i + 1, pl.ds(TOP, NJ)] = nw
                ysend[k + 1, 0, row] = nw[0:1]
                ysend[k + 1, 1, row] = nw[NJ - 1 : NJ]
                z0, z1 = take(z0, nw, i, 0), take(z1, nw, i, 1)
            return z0, z1, odd, even

        start = (zero_plane, zero_plane, (zero_acc, zero_acc), (zero_acc, zero_acc))
        z0, z1, odd, even = lax.fori_loop(0, NI, step, start)
        moments.append(odd)
        if not last:
            moments.append(even)

    row8 = rows((8, NK))
    lane8 = lanes((8, NK))
    hi = zero_acc
    lo = zero_acc
    for m, acc in enumerate(moments):
        for shift in (4, 2, 1):
            acc = df_add(acc, (pltpu.roll(acc[0], shift, 0), pltpu.roll(acc[1], shift, 0)))
        hi = jnp.where(row8 == m, acc[0], hi)
        lo = jnp.where(row8 == m, acc[1], lo)
    total = (hi, lo)
    for shift in (64, 32, 16, 8, 4, 2, 1):
        total = df_add(total, (pltpu.roll(total[0], shift, 1), pltpu.roll(total[1], shift, 1)))

    plane_to = [{"gy": lax.rem(me[1] + dy, 4), "gz": lax.rem(me[2] + dz, 4)} for dy, dz in PLANE]
    line_to = [{"gx": lax.rem(me[0] + o, 8)} for o in range(1, 8)]
    for stage, (peers, landing) in enumerate(((plane_to, a_recv0), (line_to, a_recv1))):
        a_send[stage] = jnp.where(lane8 < 64, total[0], total[1])
        copies = [
            remote(a_send.at[stage], landing.at[n], as_sem.at[stage, n], ar_sem.at[stage, n], dev)
            for n, dev in enumerate(peers)
        ]
        for c in copies:
            c.start()
        for c in copies:
            c.wait_recv()
        terms = [total]
        for n in range(len(peers)):
            x = landing[n]
            y = pltpu.roll(x, 64, 1)
            terms.append((jnp.where(lane8 < 64, x, y), jnp.where(lane8 < 64, y, x)))
        while len(terms) > 1:
            terms = [
                df_add(terms[t], terms[t + 1]) if t + 1 < len(terms) else terms[t]
                for t in range(0, len(terms), 2)
            ]
        total = terms[0]
        for c in copies:
            c.wait_send()

    nu = [(total[0][m : m + 1], total[1][m : m + 1]) for m in range(2 * ITERS)]
    coef = solve4(nu)

    def combine(parts):
        total = coef[0] * parts[0]
        for c, x in zip(coef[1:], parts[1:]):
            total = total + c * x
        return total

    pm = combine([spread_face(zrecv[k, 0]) for k in range(ITERS)])
    pf = combine([spread_face(zrecv[k, 1]) for k in range(ITERS)])
    for far in (0, NI + 1):
        pp[far, pl.ds(TOP, NJ)] = combine([w[k, far, pl.ds(TOP, NJ)] for k in range(ITERS)])

    def keep(f, i, x):
        hi, lo = split(x)
        rr = pl.ds(pl.multiple_of((i // 8) * NJ, NJ), NJ)
        cc = pl.ds(pl.multiple_of(lax.rem(i, 8) * NK, NK), NK)
        xh[f, rr, cc] = hi
        xl[f, rr, cc] = lo

    def press(i, _):
        for top, n in ((TOP - 1, 1), (TOP + NJ, 1)):
            pp[i + 1, pl.ds(top, n)] = combine([w[k, i + 1, pl.ds(top, n)] for k in range(ITERS)])
        x = combine([w[k, i + 1, pl.ds(TOP, NJ)] for k in range(ITERS)])
        pp[i + 1, pl.ds(TOP, NJ)] = x
        pst[i] = x
        keep(3, i, x)
        return 0

    lax.fori_loop(0, NI, press, 0)

    def fix(f):
        def body(i, _):
            n = ip[i + 1, pl.ds(TOP, NJ)]
            if f == 0:
                g = pp[i + 2, pl.ds(TOP, NJ)] - pp[i, pl.ds(TOP, NJ)]
                x = vx[i + 1]
            elif f == 1:
                g = pp[i + 1, pl.ds(TOP + 1, NJ)] - pp[i + 1, pl.ds(TOP - 1, NJ)]
                x = vy[i, pl.ds(TOP, NJ)]
            else:
                c = pp[i + 1, pl.ds(TOP, NJ)]
                g = ahead(c, pf, i) - behind(c, pm, i)
                x = vz[i]
            x = x - n * (0.5 * g)
            cst[f, i] = x
            keep(f, i, x)
            return 0

        lax.fori_loop(0, NI, body, 0)

    def ring(axis, way):
        a = AXES.index(axis)
        n = SIZES[a]
        to = lax.rem(me[a] + (n + way), n)
        back = lax.rem(me[a] + (n - way), n)
        opposite = lax.rem(me[a] + 2, n)
        return to, back, opposite

    def rows16(m):
        return pl.ds(pl.multiple_of(m * 16, 16), 16)

    def stage_refs(f, stage):
        axis, way = ROUTES[f]
        slot = 0 if way == 1 else 1
        if stage == 0:
            if axis == "gz":
                return axis, way, (lambda m: u.at[f, m]), za_in.at[slot], za_acc.at[slot], za_dir.at[slot], za_out.at[slot]
            return axis, way, (lambda m: u.at[f, :, :, rows16(m)]), ya_in.at[slot], ya_acc.at[slot], ya_dir.at[slot], ya_out.at[slot]
        other = "gy" if axis == "gz" else "gz"
        if axis == "gz":
            chunk = lambda m: b_src_z.at[slot, :, rows16(m)]
        else:
            chunk = lambda m: b_src_y.at[slot, m]
        return other, way, chunk, b_in.at[f], b_acc.at[f], b_dir.at[f], b_out.at[f]

    def stage_copies(f, stage):
        axis, way, chunk, r_in, r_acc, r_dir, r_out = stage_refs(f, stage)
        to, back, opposite = ring(axis, way)
        sems = lambda n: (rs_sem.at[f, stage, n], rr_sem.at[f, stage, n])
        return (
            remote(chunk(opposite), r_in, *sems(0), {axis: to}),
            remote(chunk(back), r_dir, *sems(1), {axis: back}),
            remote(r_out, r_acc, *sems(2), {axis: to}),
        )

    def stage_open(f, stage):
        far, near, _ = stage_copies(f, stage)
        far.start()
        near.start()

    def stage_relay(f, stage):
        axis, way, chunk, r_in, r_acc, r_dir, r_out = stage_refs(f, stage)
        to, back, opposite = ring(axis, way)
        far, near, relay = stage_copies(f, stage)
        far.wait_recv()
        r_out[...] = r_in[...] + chunk(to)[...]
        relay.start()

    def stage_close(f, stage):
        axis, way, chunk, r_in, r_acc, r_dir, r_out = stage_refs(f, stage)
        far, near, relay = stage_copies(f, stage)
        near.wait_recv()
        relay.wait_recv()
        return chunk(me[AXES.index(axis)])[...] + r_acc[...] + r_dir[...]

    def contract(f):
        wh, wl = wz_hi[...], wz_lo[...]
        a, b = xh[f], xl[f]
        for half in range(2):
            cols = slice(256 * half, 256 * half + 256)
            z = dot(a, wh[:, cols]) + dot(b, wh[:, cols]) + dot(a, wl[:, cols])
            for g in range(4):
                hi, lo = split(z[NJ * g : NJ * g + NJ])
                y = dot(fyt[...], jnp.concatenate([hi, hi, lo], axis=0))
                u[f, 2 * half, g] = y[:, :128]
                u[f, 2 * half + 1, g] = y[:, 128:]

    stores = [pltpu.make_async_copy(pst, out_p, out_sem.at[3])]
    stores[0].start()
    for f in ORDER:
        if f != 3:
            fix(f)
            stores.append(pltpu.make_async_copy(cst.at[f], out_c.at[f], out_sem.at[f]))
            stores[-1].start()
        contract(f)
        stage_open(f, 0)
    for f in ORDER:
        stage_relay(f, 0)
    for f in ORDER:
        whole = stage_close(f, 0)
        slot = 0 if ROUTES[f][1] == 1 else 1
        if ROUTES[f][0] == "gz":
            b_src_z[slot] = whole
        else:
            b_src_y[slot] = whole
        stage_open(f, 1)
    for f in ORDER:
        stage_relay(f, 1)
    for f in ORDER:
        whole = stage_close(f, 1)
        for g in range(4):
            ysc[16 * f : 16 * f + 16, 128 * g : 128 * g + 128] = whole[g]

    hi, lo = split(ysc[...])

    def last_dot(m, _):
        v[m] = dot(hi, k_hi[m]) + dot(lo, k_hi[m]) + dot(hi, k_lo[m])
        return 0

    lax.fori_loop(0, 8, last_dot, 0)
    copies = [
        remote(v.at[lax.rem(me[0] + o, 8)], v_recv.at[o - 1], xs_sem.at[o - 1], xr_sem.at[o - 1], line_to[o - 1])
        for o in range(1, 8)
    ]
    for c in copies:
        c.start()
    total = v[me[0]]
    for o in range(1, 8):
        copies[o - 1].wait_recv()
        total = total + v_recv[o - 1]
    for a in range(8):
        moved = total if a == 0 else pltpu.roll(total, 128 - 16 * a, 1)
        for f in range(4):
            out_core[a, f] = moved[16 * f : 16 * f + 16, :16]

    for c in copies:
        c.wait_send()
    for r in range(5):
        halo_sent(r, range(6))
    for f in ORDER:
        for stage in range(2):
            for c in stage_copies(f, stage):
                c.wait_send()
    for c in stores:
        c.wait()


def per_device(velocity, inv_density, factor_x, factor_y, factor_z):
    vmem = pl.BlockSpec(memory_space=pltpu.VMEM)
    hbm = pl.BlockSpec(memory_space=pl.ANY)
    tall = TOP + NJ + 8
    dma = pltpu.SemaphoreType.DMA
    scratch = [
        pltpu.VMEM((NI + 2, NJ, NK), F32),
        pltpu.VMEM((NI, tall, NK), F32),
        pltpu.VMEM((NI, NJ, NK), F32),
        pltpu.VMEM((NI + 2, tall, NK), F32),
        pltpu.VMEM((ITERS, NI + 2, tall, NK), F32),
        pltpu.VMEM((NI + 1, NJ, NK), F32),
        pltpu.VMEM((NI, tall, NK), F32),
        pltpu.VMEM((NI, NJ, NK), F32),
        pltpu.VMEM((NI, NJ, NK), F32),
        pltpu.VMEM((NI + 2, tall, NK), F32),
        pltpu.VMEM((NI, NJ, NK), F32),
        pltpu.VMEM((3, NI, NJ, NK), F32),
        pltpu.VMEM((ITERS, 2, NI, NK), F32),
        pltpu.VMEM((ITERS, 2, NI, NK), F32),
        pltpu.VMEM((ITERS, 2, 16, NK), F32),
        pltpu.VMEM((ITERS, 2, 16, NK), F32),
        pltpu.VMEM((2, 2, NI, NK), F32),
        pltpu.VMEM((2, 2, NI, NK), F32),
        pltpu.VMEM((2, 2, 16, NK), F32),
        pltpu.VMEM((2, 2, 16, NK), F32),
        pltpu.VMEM((2, 8, NK), F32),
        pltpu.VMEM((len(PLANE), 8, NK), F32),
        pltpu.VMEM((7, 8, NK), F32),
        pltpu.VMEM((1024, 512), BF16),
        pltpu.VMEM((1024, 512), BF16),
        pltpu.VMEM((64, 192), BF16),
        pltpu.VMEM((8, 512, 128), BF16),
        pltpu.VMEM((8, 512, 128), BF16),
        pltpu.VMEM((4, 256, 1024), BF16),
        pltpu.VMEM((4, 256, 1024), BF16),
        pltpu.VMEM((4, 4, 4, 64, 128), F32),
    ]
    scratch += [pltpu.VMEM((2, 4, 64, 128), F32)] * 4
    scratch += [pltpu.VMEM((2, 4, 4, 16, 128), F32)] * 4
    scratch += [pltpu.VMEM((2, 4, 64, 128), F32), pltpu.VMEM((2, 4, 4, 16, 128), F32)]
    scratch += [pltpu.VMEM((4, 4, 16, 128), F32)] * 4
    scratch += [
        pltpu.VMEM((64, 512), F32),
        pltpu.VMEM((8, 64, 128), F32),
        pltpu.VMEM((7, 64, 128), F32),
        dma((4,)),
        dma((4,)),
        dma((5, 6, 2)),
        dma((5, 6, 2)),
        dma((2, len(PLANE))),
        dma((2, len(PLANE))),
        dma((4, 2, 3)),
        dma((4, 2, 3)),
        dma((7,)),
        dma((7,)),
    ]
    return pl.pallas_call(
        kernel,
        out_shape=(
            jax.ShapeDtypeStruct(inv_density.shape, F32),
            jax.ShapeDtypeStruct(velocity.shape, F32),
            jax.ShapeDtypeStruct((8, 4, 16, 16), F32),
        ),
        in_specs=[hbm, hbm, vmem, vmem, vmem],
        out_specs=(hbm, hbm, vmem),
        scratch_shapes=scratch,
        compiler_params=pltpu.CompilerParams(
            collective_id=0, has_side_effects=True, vmem_limit_bytes=60 * 1024 * 1024
        ),
    )(velocity, inv_density, factor_x, factor_y, factor_z)


def solution(mesh):
    placed = (
        P(None, "gx", "gy", "gz"),
        P("gx", "gy", "gz"),
        P("gx", None),
        P("gy", None),
        P("gz", None),
    )
    return jax.shard_map(
        per_device,
        mesh=mesh,
        in_specs=placed,
        out_specs=(P("gx", "gy", "gz"), P(None, "gx", "gy", "gz"), P("gx", None, "gy", "gz")),
        check_vma=False,
    )
```

time: 1020 us -> 125 us (0.12)
  blocking collectives: 458 us -> 0 us
  waiting for transfers between devices: 160 us -> 0 us
  local copies, waits for them, and re-layouts: 126 us -> 8.51 us
  Pallas kernels: 0 us -> 115 us
  starting transfers between devices: 103 us -> 0 us
  other arithmetic: 86 us -> 0 us
  matrix products: 53.1 us -> 0 us
  between operations: 24.4 us -> 0.64 us
    psum x7 -> x0, blocking collectives: 458 us -> none  [the longest x4 261 us: residual_product(): return lax.psum(jnp.sum(residual * precond), ('gx', 'gy', 'gz'))]
    unnamed x2 -> x0, waiting for transfers between devices: 147 us -> none
    pallas_call x0 -> x1, Pallas kernels: none -> 115 us  [per_device(): pl.pallas_call(kernel, out_shape=(jax.ShapeDtypeStruct(inv_density.shape,...]
    ppermute x36 -> x0, starting transfers between devices: 103 us -> none  [the longest x18 70.9 us: padded_2(): lax.ppermute(tail, axis, [(i, (i + 1) % count) for i in range(ends)])]
    dot_general x3 -> x0, matrix products: 53.1 us -> none  [the longest x1 28.8 us: per_device(): jnp.einsum('PQafbk,kRc->PQRafbc', second, split_z, precision=HIGHEST)]
    reduce_sum x7 -> x0, other arithmetic: 50.2 us -> none  [the longest x4 39 us: per_device(): alpha = product / lax.psum(jnp.sum(direction * image), ('gx', 'gy', 'gz'))]
    slice x23 -> x0, local copies, waits for them, and re-layouts: 45.4 us -> none  [the longest x11 24.6 us: padded_2(): head = lax.slice_in_dim(cells, 0, width, axis=dim)]
    reshape x2 -> x0, local copies, waits for them, and re-layouts: 29.2 us -> none  [the longest x1 28.3 us: per_device(): flat = third.reshape(groups_x * groups_y * groups_z, -1)]
  transfers between devices with their start and end apart: 37 -> 0, of which waited for: 14 -> 0; matrix products, arithmetic and copies ran while one was open for 4% -> 0% of each run, Pallas kernels for 0% -> 0%
where the time goes in v1:
time: 125 us; the launch traced here: 124 us
  Pallas kernels  115 us (92%)
  local copies, waits for them, and re-layouts  8.51 us (7%)
    pallas_call x1, Pallas kernels, per_device(): pl.pallas_call(kernel, out_shape=(jax.ShapeDtypeStruct(inv_density.shape,...  115 us
    unnamed x6, local copies, waits for them, and re-layouts  8.51 us

profile of v1, /device:TPU:1, one launch (start us, length us, event | category | flops | bytes accessed | tf_op | source)
XLA Modules:
  0.0 124.3 jit_solution(2912940517480376243)
XLA Ops:
  0.6 1.5 %copy.8.fz = f32[128,64]{1,0:T(8,128)} copy(f32[128,64]{0,1:T(8,128)} %param.9) | data formatting | bytes 65536 | tf_op args[4]
  2.1 115.2 %shard_map.76 = (f32[32,64,128]{2,1,0:T(8,128)}, f32[3,32,64,128]{3,2,1,0:T(8,128)}, f32[8,4,16,16]{3,2,1,0:T(8,128)}) custom-call(f32[3,32,64,128]{3,2,1,0:T(8,128)} %vel.1, f32[32,64,128]{2,1,0:T(8,128)} %inv.1, f32[32,64]{1,0:T(8,128)} %fx.1, f32[64,64]{1,0:T(8,128)} %fy.1, f32[128,64]{1,0:T(8,128)} %copy.8.fz), custom_call_target="tpu_custom_call" | custom-call | tf_op jit(solution)/shard_map/pallas_call | solution.py:687
  117.3 2.3 %copy.12 = f32[32,64,128]{2,1,0:T(8,128)} copy(f32[32,64,128]{2,1,0:T(8,128)} %get-tuple-element.6) | data formatting | bytes 2097152
  119.6 0.0 copy-start
  119.6 4.0 %copy.13 = f32[3,32,64,128]{3,2,1,0:T(8,128)} copy(f32[3,32,64,128]{3,2,1,0:T(8,128)} %get-tuple-element.7) | data formatting | bytes 6291456
  123.6 0.0 copy-done
  123.6 0.7 copy.14
Async XLA Ops:
  119.6 4.0 %copy-start = (f32[8,4,16,16]{3,2,1,0:T(8,128)S(1)}, f32[8,4,16,16]{3,2,1,0:T(8,128)}, u32[]{:S(2)}) copy-start(f32[8,4,16,16]{3,2,1,0:T(8,128)} %get-tuple-element.8) | copy-start | bytes 98308

commit v2 on v1

--- a/solution.py
+++ b/solution.py
@@ -113,43 +113,18 @@
     return lax.dot_general(a, b, (((1,), (0,)), ((), ())), preferred_element_type=F32)
 
 
-def squeeze_face(face):
-    lane = lanes((8, 128))
-    halves_ = []
-    for h in range(2):
-        acc = face[32 * h : 32 * h + 8]
-        for q in range(1, 4):
-            part = face[32 * h + 8 * q : 32 * h + 8 * q + 8]
-            acc = jnp.where(lane // 32 == q, pltpu.roll(part, 32 * q, 1), acc)
-        halves_.append(acc)
-    return jnp.concatenate(halves_, axis=0)
-
-
-def spread_face(packed):
-    parts = []
-    for h in range(2):
-        for q in range(4):
-            part = packed[8 * h : 8 * h + 8]
-            parts.append(part if q == 0 else pltpu.roll(part, 128 - 32 * q, 1))
-    return jnp.concatenate(parts, axis=0)
-
-
-def fold(x):
-    t = [x[8 * q : 8 * q + 8] for q in range(8)]
-    return ((t[0] + t[1]) + (t[2] + t[3])) + ((t[4] + t[5]) + (t[6] + t[7]))
-
-
 def kernel(
     vel, inv, fx, fy, fz,
     out_p, out_c, out_core,
-    vx, vy, vz, ip, w, cx, cy, cz, dinv, pp, pst, cst,
-    ysend, yrecv, zsend, zrecv, ysend0, yrecv0, zsend0, zrecv0,
+    vx, vy, vz, ip, w0, w1, w2, w3, cx, cy, cz, dinv, pp, pst, cst,
+    zsend, zrecv, zsend0, zrecv0,
     a_send, a_recv0, a_recv1,
     wz_hi, wz_lo, fyt, k_hi, k_lo, xh, xl, u,
     za_in, za_acc, za_dir, za_out, ya_in, ya_acc, ya_dir, ya_out,
     b_src_z, b_src_y, b_in, b_acc, b_dir, b_out, ysc, v, v_recv,
     in_sem, out_sem, hs_sem, hr_sem, as_sem, ar_sem, rs_sem, rr_sem, xs_sem, xr_sem,
 ):
+    w = (w0, w1, w2, w3)
     me = [lax.axis_index(a) for a in AXES]
     has = []
     for a in range(3):
@@ -165,7 +140,8 @@
             src_ref=src, dst_ref=dst, send_sem=ss, recv_sem=rs, device_id=dev, device_id_type=MESH
         )
 
-    lane = lanes((NJ, NK))
+    lane = lanes((8, NK))
+    pending = []
 
     loads = [
         pltpu.make_async_copy(inv, ip.at[pl.ds(1, NI), pl.ds(TOP, NJ)], in_sem.at[0]),
@@ -177,70 +153,70 @@
         c.start()
 
     barrier = pltpu.get_barrier_semaphore()
-    for o in range(1, 8):
-        pl.semaphore_signal(barrier, inc=1, device_id={"gx": lax.rem(me[0] + o, 8)}, device_id_type=MESH)
-    for dy, dz in PLANE:
-        pl.semaphore_signal(
-            barrier, inc=1,
-            device_id={"gy": lax.rem(me[1] + dy, 4), "gz": lax.rem(me[2] + dz, 4)},
-            device_id_type=MESH,
-        )
+    for side in range(6):
+        pl.semaphore_signal(barrier, inc=1, device_id=neighbour(side), device_id_type=MESH)
 
     zero_plane = jnp.zeros((NJ, NK), F32)
+    zero_row = jnp.zeros((1, NK), F32)
     for s in range(2):
         far = (0, NI + 1)[s]
+        edge = (TOP - 1, TOP + NJ)[s]
 
         @pl.when(jnp.logical_not(has[s]))
         def _():
             vx[far] = zero_plane
-            ip[far, pl.ds(TOP, NJ)] = zero_plane
-            for k in range(ITERS):
-                w[k, far, pl.ds(TOP, NJ)] = zero_plane
+            for ref in (ip,) + w:
+                ref[far, pl.ds(TOP, NJ)] = zero_plane
 
         @pl.when(jnp.logical_not(has[2 + s]))
         def _():
-            yrecv0[s] = jnp.zeros((2, NI, NK), F32)
-            for k in range(ITERS):
-                yrecv[k, s] = jnp.zeros((NI, NK), F32)
+            for i in range(NI):
+                vy[i, pl.ds(edge, 1)] = zero_row
+                for ref in (ip,) + w:
+                    ref[i + 1, pl.ds(edge, 1)] = zero_row
 
         @pl.when(jnp.logical_not(has[4 + s]))
         def _():
-            zrecv0[s] = jnp.zeros((2, 16, NK), F32)
+            zrecv0[s] = jnp.zeros((2, 32, NK), F32)
             for k in range(ITERS):
-                zrecv[k, s] = jnp.zeros((16, NK), F32)
-
-    pl.semaphore_wait(barrier, 7 + len(PLANE))
+                zrecv[k, s] = jnp.zeros((32, NK), F32)
+
+    pl.semaphore_wait(barrier, 6)
 
     def halo(r, side, landing):
-        near = (1, NI)[side % 2]
-        far = (0, NI + 1)[landing % 2]
         s, t = side % 2, landing % 2
         ax = side // 2
-        if r == 0:
-            if ax == 0:
+        planes = pl.ds(1, NI)
+        if ax == 0:
+            near, far = (1, NI)[s], (0, NI + 1)[t]
+            if r == 0:
                 edge = (0, NI - 1)[s]
                 pairs = [
                     (vel.at[0, edge], vx.at[far]),
                     (inv.at[edge], ip.at[far, pl.ds(TOP, NJ)]),
                 ]
-            elif ax == 1:
-                pairs = [(ysend0.at[s], yrecv0.at[t])]
             else:
-                pairs = [(zsend0.at[s], zrecv0.at[t])]
+                ref = w[r - 1]
+                pairs = [(ref.at[near, pl.ds(TOP, NJ)], ref.at[far, pl.ds(TOP, NJ)])]
+        elif ax == 1:
+            near, far = (TOP, TOP + NJ - 1)[s], (TOP - 1, TOP + NJ)[t]
+            if r == 0:
+                edge = (0, NJ - 1)[s]
+                pairs = [(vel.at[1, :, edge], vy.at[:, far]), (inv.at[:, edge], ip.at[planes, far])]
+            else:
+                ref = w[r - 1]
+                pairs = [(ref.at[planes, near], ref.at[planes, far])]
+        elif r == 0:
+            pairs = [(zsend0, zrecv0.at[t])]
         else:
-            k = r - 1
-            if ax == 0:
-                pairs = [(w.at[k, near, pl.ds(TOP, NJ)], w.at[k, far, pl.ds(TOP, NJ)])]
-            elif ax == 1:
-                pairs = [(ysend.at[k, s], yrecv.at[k, t])]
-            else:
-                pairs = [(zsend.at[k, s], zrecv.at[k, t])]
+            pairs = [(zsend.at[r - 1], zrecv.at[r - 1, t])]
         return [
             remote(a, b, hs_sem.at[r, side, n], hr_sem.at[r, landing, n], neighbour(side))
             for n, (a, b) in enumerate(pairs)
         ]
 
     def halo_start(r, sides):
+        pending.append(lambda: halo_sent(r, sides))
         for side in sides:
             @pl.when(has[side])
             def _():
@@ -261,36 +237,55 @@
                 for c in halo(r, side, side ^ 1):
                     c.wait_send()
 
-    halo_start(0, (0, 1))
-
-    def take(acc, x, i, edge):
-        moved = pltpu.roll(x, i if edge == 0 else i + 1, 1)
-        return jnp.where(lane == i, moved, acc)
-
-    for c in loads[:3]:
+    halo_start(0, range(4))
+
+    def tiles(x):
+        return [x[8 * q : 8 * q + 8] for q in range(x.shape[0] // 8)]
+
+    def pack(acc, x, i):
+        out = list(acc)
+        for q, part in enumerate(x):
+            moved = pltpu.roll(part, 2 * i + 1 + 64 * (q // 4), 1)
+            out[q % 4] = jnp.where(lane // 2 == i + 32 * (q // 4), moved, out[q % 4])
+        return out
+
+    def unpack(faces, i):
+        return [pltpu.roll(faces[q % 4], lax.rem(255 - 2 * i - 64 * (q // 4), 128), 1) for q in range(8)]
+
+    def ahead(x, ends):
+        return [pltpu.roll(jnp.where(lane == 0, e, a), NK - 1, 1) for a, e in zip(x, ends)]
+
+    def behind(x, ends):
+        return [pltpu.roll(jnp.where(lane == NK - 1, e, a), 1, 1) for a, e in zip(x, ends)]
+
+    first_half = lax.broadcasted_iota(jnp.int32, (8, NK), 1) % 2 == 1
+
+    def merge(plus, minus):
+        return [jnp.where(first_half, a, b) for a, b in zip(plus, minus)]
+
+    GROUP = 4
+    no_faces = [jnp.zeros((8, NK), F32)] * 4
+    zero_acc = jnp.zeros((8, NK), F32)
+
+    for c in loads[:2]:
         c.wait()
 
-    def face0(i, carry):
-        u0, u1, n0, n1 = carry
-        a = vz[i]
-        b = ip[i + 1, pl.ds(TOP, NJ)]
-        row = pl.ds(i, 1)
-        ysend0[0, 0, row] = vy[i, pl.ds(TOP, 1)]
-        ysend0[1, 0, row] = vy[i, pl.ds(TOP + NJ - 1, 1)]
-        ysend0[0, 1, row] = b[0:1]
-        ysend0[1, 1, row] = b[NJ - 1 : NJ]
-        return take(u0, a, i, 0), take(u1, a, i, 1), take(n0, b, i, 0), take(n1, b, i, 1)
-
-    u0, u1, n0, n1 = lax.fori_loop(0, NI, face0, (zero_plane,) * 4, unroll=2)
-    zsend0[0, 0] = squeeze_face(u0)
-    zsend0[1, 0] = squeeze_face(u1)
-    zsend0[0, 1] = squeeze_face(n0)
-    zsend0[1, 1] = squeeze_face(n1)
-    halo_start(0, (2, 3, 4, 5))
-    loads[3].wait()
-
-    z64 = jnp.zeros((NK, 64), F32)
-    fzp = jnp.concatenate([fz[...], z64], axis=1)
+    def face0(t, carry):
+        a, b = carry
+        for g in range(GROUP):
+            i = t * GROUP + g
+            a = pack(a, tiles(vz[i]), i)
+            b = pack(b, tiles(ip[i + 1, pl.ds(TOP, NJ)]), i)
+        return a, b
+
+    fu, fn = lax.fori_loop(0, NI // GROUP, face0, (no_faces, no_faces))
+    zsend0[0] = jnp.concatenate(fu, axis=0)
+    zsend0[1] = jnp.concatenate(fn, axis=0)
+    halo_start(0, (4, 5))
+    for c in loads[2:]:
+        c.wait()
+
+    fzp = jnp.concatenate([fz[...], jnp.zeros((64, NK), F32)], axis=0).T
     lane_k = lanes((NK, 128))
 
     def build_z(i8, _):
@@ -321,90 +316,94 @@
 
     halo_wait(0, range(6))
 
-    def ahead(x, face, i):
-        return pltpu.roll(jnp.where(lane == 0, pltpu.roll(face, lax.rem(NK - i, NK), 1), x), NK - 1, 1)
-
-    def behind(x, face, i):
-        return pltpu.roll(jnp.where(lane == NK - 1, pltpu.roll(face, NK - 1 - i, 1), x), 1, 1)
-
-    um, up = spread_face(zrecv0[0, 0]), spread_face(zrecv0[1, 0])
-    nm, np_ = spread_face(zrecv0[0, 1]), spread_face(zrecv0[1, 1])
-    czb = 0.5 * (n0 + nm)
-    zero_acc = jnp.zeros((8, NK), F32)
-
-    def accumulate(acc, x):
-        s, e = two_sum(acc[0], fold(x))
+    fu = merge(tiles(zrecv0[1, 0]), tiles(zrecv0[0, 0]))
+    nminus = tiles(zrecv0[0, 1])
+    czb = [0.5 * (a + pltpu.roll(b, NK - 1, 1)) for a, b in zip(nminus, fn)]
+    fn = merge(tiles(zrecv0[1, 1]), nminus)
+
+    def accumulate(acc, parts):
+        while len(parts) > 1:
+            parts = [parts[n] + parts[n + 1] for n in range(0, len(parts), 2)]
+        s, e = two_sum(acc[0], parts[0])
         return s, acc[1] + e
 
-    def first(i, carry):
-        z0, z1, acc = carry
-        row = pl.ds(i, 1)
-        ip[i + 1, pl.ds(TOP - 1, 1)] = yrecv0[0, 1, row]
-        ip[i + 1, pl.ds(TOP + NJ, 1)] = yrecv0[1, 1, row]
-        vy[i, pl.ds(TOP - 1, 1)] = yrecv0[0, 0, row]
-        vy[i, pl.ds(TOP + NJ, 1)] = yrecv0[1, 0, row]
-        n = ip[i + 1, pl.ds(TOP, NJ)]
-        xb = 0.5 * (n + ip[i, pl.ds(TOP, NJ)])
-        xf = 0.5 * (n + ip[i + 2, pl.ds(TOP, NJ)])
-        yb = 0.5 * (n + ip[i + 1, pl.ds(TOP - 1, NJ)])
-        yf = 0.5 * (n + ip[i + 1, pl.ds(TOP + 1, NJ)])
-        zb = 0.5 * (n + behind(n, nm, i))
-        zf = 0.5 * (n + ahead(n, np_, i))
-        cx[i] = xb
-        cx[i + 1] = xf
-        cy[i, pl.ds(TOP, NJ)] = yf
-        cy[i, pl.ds(TOP - 1, 1)] = yb[0:1]
-        cz[i] = zf
-        d = SHIFT + xf + xb + yf + yb + zf + zb
-        a = vz[i]
-        div = 0.5 * (vx[i + 2] - vx[i])
-        div = div + 0.5 * (vy[i, pl.ds(TOP + 1, NJ)] - vy[i, pl.ds(TOP - 1, NJ)])
-        div = div + 0.5 * (ahead(a, up, i) - behind(a, um, i))
-        b = -div
-        di = 1.0 / d
-        dinv[i] = di
-        w0 = b * di
-        w[0, i + 1, pl.ds(TOP, NJ)] = w0
-        ysend[0, 0, row] = w0[0:1]
-        ysend[0, 1, row] = w0[NJ - 1 : NJ]
-        return take(z0, w0, i, 0), take(z1, w0, i, 1), accumulate(acc, b * w0)
-
-    z0, z1, acc = lax.fori_loop(0, NI, first, (zero_plane, zero_plane, (zero_acc, zero_acc)))
+    def mul(a, b):
+        return [x * y for x, y in zip(a, b)]
+
+    def join(x):
+        return jnp.concatenate(x, axis=0)
+
+    def first(t, carry):
+        faces, acc = carry
+        terms = []
+        for g in range(GROUP):
+            i = t * GROUP + g
+            n = ip[i + 1, pl.ds(TOP, NJ)]
+            xf = ip[i + 2, pl.ds(TOP, NJ)]
+            yf = ip[i + 1, pl.ds(TOP + 1, NJ)]
+            xb = ip[i, pl.ds(TOP, NJ)]
+            yb = ip[i + 1, pl.ds(TOP - 1, NJ)]
+            nt = tiles(n)
+            ends = unpack(fn, i)
+            zb = join(behind(nt, ends))
+            zf = join(ahead(nt, ends))
+            cx[i + 1] = 0.5 * (n + xf)
+            cy[i, pl.ds(TOP, NJ)] = 0.5 * (n + yf)
+            cy[i, pl.ds(TOP - 1, 1)] = 0.5 * (n + yb)[0:1]
+            cz[i] = 0.5 * (n + zf)
+            d = (SHIFT + 3.0 * n) + 0.5 * (((xf + xb) + (yf + yb)) + (zf + zb))
+            at = tiles(vz[i])
+            ends = unpack(fu, i)
+            div = (vx[i + 2] - vx[i]) + (vy[i, pl.ds(TOP + 1, NJ)] - vy[i, pl.ds(TOP - 1, NJ)])
+            div = div + (join(ahead(at, ends)) - join(behind(at, ends)))
+            b = -0.5 * div
+            di = 1.0 / d
+            dinv[i] = di
+            new = b * di
+            w0[i + 1, pl.ds(TOP, NJ)] = new
+            faces = pack(faces, tiles(new), i)
+            terms += tiles(b * new)
+        return faces, accumulate(acc, terms)
+
+    cx[0] = 0.5 * (ip[0, pl.ds(TOP, NJ)] + ip[1, pl.ds(TOP, NJ)])
+    faces, acc = lax.fori_loop(0, NI // GROUP, first, (no_faces, (zero_acc, zero_acc)))
     moments = [acc]
 
-    faces = []
     for k in range(ITERS):
-        zsend[k, 0] = squeeze_face(z0)
-        zsend[k, 1] = squeeze_face(z1)
+        zsend[k] = join(faces)
         halo_start(k + 1, range(6))
         halo_wait(k + 1, range(6))
-        wm, wp = spread_face(zrecv[k, 0]), spread_face(zrecv[k, 1])
-        flux = czb * wm
+        after = tiles(zrecv[k, 1])
+        flux = merge(after, mul(czb, tiles(zrecv[k, 0])))
         last = k == ITERS - 1
-
-        def step(i, carry):
-            z0, z1, odd, even = carry
-            row = pl.ds(i, 1)
-            w[k, i + 1, pl.ds(TOP - 1, 1)] = yrecv[k, 0, row]
-            w[k, i + 1, pl.ds(TOP + NJ, 1)] = yrecv[k, 1, row]
-            c = w[k, i + 1, pl.ds(TOP, NJ)]
-            f = cz[i]
-            bw = cx[i] * w[k, i, pl.ds(TOP, NJ)] + cx[i + 1] * w[k, i + 2, pl.ds(TOP, NJ)]
-            bw = bw + cy[i, pl.ds(TOP - 1, NJ)] * w[k, i + 1, pl.ds(TOP - 1, NJ)]
-            bw = bw + cy[i, pl.ds(TOP, NJ)] * w[k, i + 1, pl.ds(TOP + 1, NJ)]
-            bw = bw + (f * ahead(c, wp, i) + behind(f * c, flux, i))
-            odd = accumulate(odd, c * bw)
+        here = w[k]
+        there = None if last else w[k + 1]
+
+        def step(t, carry):
+            faces, odd, even = carry
+            t_odd, t_even = [], []
+            for g in range(GROUP):
+                i = t * GROUP + g
+                c = here[i + 1, pl.ds(TOP, NJ)]
+                f = cz[i]
+                bw = cx[i] * here[i, pl.ds(TOP, NJ)] + cx[i + 1] * here[i + 2, pl.ds(TOP, NJ)]
+                bw = bw + cy[i, pl.ds(TOP - 1, NJ)] * here[i + 1, pl.ds(TOP - 1, NJ)]
+                bw = bw + cy[i, pl.ds(TOP, NJ)] * here[i + 1, pl.ds(TOP + 1, NJ)]
+                ends = unpack(flux, i)
+                bw = bw + (f * join(ahead(tiles(c), ends)) + join(behind(tiles(f * c), ends)))
+                t_odd += tiles(c * bw)
+                if not last:
+                    new = bw * dinv[i]
+                    t_even += tiles(bw * new)
+                    there[i + 1, pl.ds(TOP, NJ)] = new
+                    faces = pack(faces, tiles(new), i)
+            odd = accumulate(odd, t_odd)
             if not last:
-                nw = bw * dinv[i]
-                even = accumulate(even, bw * nw)
-                w[k + 1, i + 1, pl.ds(TOP, NJ)] = nw
-                ysend[k + 1, 0, row] = nw[0:1]
-                ysend[k + 1, 1, row] = nw[NJ - 1 : NJ]
-                z0, z1 = take(z0, nw, i, 0), take(z1, nw, i, 1)
-            return z0, z1, odd, even
-
-        start = (zero_plane, zero_plane, (zero_acc, zero_acc), (zero_acc, zero_acc))
-        z0, z1, odd, even = lax.fori_loop(0, NI, step, start)
+                even = accumulate(even, t_even)
+            return faces, odd, even
+
+        start = (no_faces, (zero_acc, zero_acc), (zero_acc, zero_acc))
+        faces, odd, even = lax.fori_loop(0, NI // GROUP, step, start)
         moments.append(odd)
         if not last:
             moments.append(even)
@@ -457,10 +456,10 @@
             total = total + c * x
         return total
 
-    pm = combine([spread_face(zrecv[k, 0]) for k in range(ITERS)])
-    pf = combine([spread_face(zrecv[k, 1]) for k in range(ITERS)])
+    pe = combine([join(merge(tiles(zrecv[k, 1]), tiles(zrecv[k, 0]))) for k in range(ITERS)])
+    pe = tiles(pe)
     for far in (0, NI + 1):
-        pp[far, pl.ds(TOP, NJ)] = combine([w[k, far, pl.ds(TOP, NJ)] for k in range(ITERS)])
+        pp[far, pl.ds(TOP, NJ)] = combine([ref[far, pl.ds(TOP, NJ)] for ref in w])
 
     def keep(f, i, x):
         hi, lo = split(x)
@@ -469,36 +468,41 @@
         xh[f, rr, cc] = hi
         xl[f, rr, cc] = lo
 
-    def press(i, _):
-        for top, n in ((TOP - 1, 1), (TOP + NJ, 1)):
-            pp[i + 1, pl.ds(top, n)] = combine([w[k, i + 1, pl.ds(top, n)] for k in range(ITERS)])
-        x = combine([w[k, i + 1, pl.ds(TOP, NJ)] for k in range(ITERS)])
-        pp[i + 1, pl.ds(TOP, NJ)] = x
-        pst[i] = x
-        keep(3, i, x)
+    def press(t, _):
+        for g in range(GROUP):
+            i = t * GROUP + g
+            for top, n in ((TOP - 1, 1), (TOP + NJ, 1)):
+                pp[i + 1, pl.ds(top, n)] = combine([ref[i + 1, pl.ds(top, n)] for ref in w])
+            x = combine([ref[i + 1, pl.ds(TOP, NJ)] for ref in w])
+            pp[i + 1, pl.ds(TOP, NJ)] = x
+            pst[i] = x
+            keep(3, i, x)
         return 0
 
-    lax.fori_loop(0, NI, press, 0)
+    lax.fori_loop(0, NI // GROUP, press, 0)
 
     def fix(f):
-        def body(i, _):
-            n = ip[i + 1, pl.ds(TOP, NJ)]
-            if f == 0:
-                g = pp[i + 2, pl.ds(TOP, NJ)] - pp[i, pl.ds(TOP, NJ)]
-                x = vx[i + 1]
-            elif f == 1:
-                g = pp[i + 1, pl.ds(TOP + 1, NJ)] - pp[i + 1, pl.ds(TOP - 1, NJ)]
-                x = vy[i, pl.ds(TOP, NJ)]
-            else:
-                c = pp[i + 1, pl.ds(TOP, NJ)]
-                g = ahead(c, pf, i) - behind(c, pm, i)
-                x = vz[i]
-            x = x - n * (0.5 * g)
-            cst[f, i] = x
-            keep(f, i, x)
+        def body(t, _):
+            for g in range(GROUP):
+                i = t * GROUP + g
+                n = ip[i + 1, pl.ds(TOP, NJ)]
+                if f == 0:
+                    g_ = pp[i + 2, pl.ds(TOP, NJ)] - pp[i, pl.ds(TOP, NJ)]
+                    x = vx[i + 1]
+                elif f == 1:
+                    g_ = pp[i + 1, pl.ds(TOP + 1, NJ)] - pp[i + 1, pl.ds(TOP - 1, NJ)]
+                    x = vy[i, pl.ds(TOP, NJ)]
+                else:
+                    c = tiles(pp[i + 1, pl.ds(TOP, NJ)])
+                    ends = unpack(pe, i)
+                    g_ = join(ahead(c, ends)) - join(behind(c, ends))
+                    x = vz[i]
+                x = x - n * (0.5 * g_)
+                cst[f, i] = x
+                keep(f, i, x)
             return 0
 
-        lax.fori_loop(0, NI, body, 0)
+        lax.fori_loop(0, NI // GROUP, body, 0)
 
     def ring(axis, way):
         a = AXES.index(axis)
@@ -539,6 +543,8 @@
         far, near, _ = stage_copies(f, stage)
         far.start()
         near.start()
+        pending.append(far.wait_send)
+        pending.append(near.wait_send)
 
     def stage_relay(f, stage):
         axis, way, chunk, r_in, r_acc, r_dir, r_out = stage_refs(f, stage)
@@ -547,6 +553,7 @@
         far.wait_recv()
         r_out[...] = r_in[...] + chunk(to)[...]
         relay.start()
+        pending.append(relay.wait_send)
 
     def stage_close(f, stage):
         axis, way, chunk, r_in, r_acc, r_dir, r_out = stage_refs(f, stage)
@@ -569,11 +576,13 @@
 
     stores = [pltpu.make_async_copy(pst, out_p, out_sem.at[3])]
     stores[0].start()
+    pending.append(stores[0].wait)
     for f in ORDER:
         if f != 3:
             fix(f)
             stores.append(pltpu.make_async_copy(cst.at[f], out_c.at[f], out_sem.at[f]))
             stores[-1].start()
+            pending.append(stores[-1].wait)
         contract(f)
         stage_open(f, 0)
     for f in ORDER:
@@ -606,6 +615,7 @@
     ]
     for c in copies:
         c.start()
+        pending.append(c.wait_send)
     total = v[me[0]]
     for o in range(1, 8):
         copies[o - 1].wait_recv()
@@ -615,16 +625,8 @@
         for f in range(4):
             out_core[a, f] = moved[16 * f : 16 * f + 16, :16]
 
-    for c in copies:
-        c.wait_send()
-    for r in range(5):
-        halo_sent(r, range(6))
-    for f in ORDER:
-        for stage in range(2):
-            for c in stage_copies(f, stage):
-                c.wait_send()
-    for c in stores:
-        c.wait()
+    for wait in pending:
+        wait()
 
 
 def per_device(velocity, inv_density, factor_x, factor_y, factor_z):
@@ -637,7 +639,10 @@
         pltpu.VMEM((NI, tall, NK), F32),
         pltpu.VMEM((NI, NJ, NK), F32),
         pltpu.VMEM((NI + 2, tall, NK), F32),
-        pltpu.VMEM((ITERS, NI + 2, tall, NK), F32),
+        pltpu.VMEM((NI + 2, tall, NK), F32),
+        pltpu.VMEM((NI + 2, tall, NK), F32),
+        pltpu.VMEM((NI + 2, tall, NK), F32),
+        pltpu.VMEM((NI + 2, tall, NK), F32),
         pltpu.VMEM((NI + 1, NJ, NK), F32),
         pltpu.VMEM((NI, tall, NK), F32),
         pltpu.VMEM((NI, NJ, NK), F32),
@@ -645,14 +650,10 @@
         pltpu.VMEM((NI + 2, tall, NK), F32),
         pltpu.VMEM((NI, NJ, NK), F32),
         pltpu.VMEM((3, NI, NJ, NK), F32),
-        pltpu.VMEM((ITERS, 2, NI, NK), F32),
-        pltpu.VMEM((ITERS, 2, NI, NK), F32),
-        pltpu.VMEM((ITERS, 2, 16, NK), F32),
-        pltpu.VMEM((ITERS, 2, 16, NK), F32),
-        pltpu.VMEM((2, 2, NI, NK), F32),
-        pltpu.VMEM((2, 2, NI, NK), F32),
-        pltpu.VMEM((2, 2, 16, NK), F32),
-        pltpu.VMEM((2, 2, 16, NK), F32),
+        pltpu.VMEM((ITERS, 32, NK), F32),
+        pltpu.VMEM((ITERS, 2, 32, NK), F32),
+        pltpu.VMEM((2, 32, NK), F32),
+        pltpu.VMEM((2, 2, 32, NK), F32),
         pltpu.VMEM((2, 8, NK), F32),
         pltpu.VMEM((len(PLANE), 8, NK), F32),
         pltpu.VMEM((7, 8, NK), F32),
@@ -697,7 +698,7 @@
         compiler_params=pltpu.CompilerParams(
             collective_id=0, has_side_effects=True, vmem_limit_bytes=60 * 1024 * 1024
         ),
-    )(velocity, inv_density, factor_x, factor_y, factor_z)
+    )(velocity, inv_density, factor_x, factor_y, factor_z.T)
 
 
 def solution(mesh):

time: 125 us -> 90.2 us (0.72)
  Pallas kernels: 115 us -> 82.4 us
  local copies, waits for them, and re-layouts: 8.51 us -> 7.02 us
    pallas_call x1, Pallas kernels: 115 us -> 82.4 us  [per_device(): pl.pallas_call(kernel, out_shape=(jax.ShapeDtypeStruct(inv_density.shape,...]
    unnamed x6 -> x5, local copies, waits for them, and re-layouts: 8.51 us -> 7.02 us
where the time goes in v2:
time: 90.2 us; the launch traced here: 90 us
  Pallas kernels  82.4 us (91%)
  local copies, waits for them, and re-layouts  7.02 us (8%)
    pallas_call x1, Pallas kernels, per_device(): pl.pallas_call(kernel, out_shape=(jax.ShapeDtypeStruct(inv_density.shape,...  82.4 us
    unnamed x5, local copies, waits for them, and re-layouts  7.02 us

profile of v2, /device:TPU:1, one launch (start us, length us, event | category | flops | bytes accessed | tf_op | source)
XLA Modules:
  0.0 90.0 jit_solution(10540334741351588816)
XLA Ops:
  0.6 82.4 %shard_map.76 = (f32[32,64,128]{2,1,0:T(8,128)}, f32[3,32,64,128]{3,2,1,0:T(8,128)}, f32[8,4,16,16]{3,2,1,0:T(8,128)}) custom-call(f32[3,32,64,128]{3,2,1,0:T(8,128)} %vel.1, f32[32,64,128]{2,1,0:T(8,128)} %inv.1, f32[32,64]{1,0:T(8,128)} %fx.1, f32[64,64]{1,0:T(8,128)} %fy.1, f32[64,128]{1,0:T(8,128)} %bitcast.1), custom_call_target="tpu_custom_call" | custom-call | tf_op jit(solution)/shard_map/pallas_call | solution.py:688
  83.0 2.3 %copy.11 = f32[32,64,128]{2,1,0:T(8,128)} copy(f32[32,64,128]{2,1,0:T(8,128)} %get-tuple-element.6) | data formatting | bytes 2097152
  85.3 0.0 copy-start
  85.3 4.0 %copy.12 = f32[3,32,64,128]{3,2,1,0:T(8,128)} copy(f32[3,32,64,128]{3,2,1,0:T(8,128)} %get-tuple-element.7) | data formatting | bytes 6291456
  89.3 0.0 copy-done
  89.3 0.7 copy.13
Async XLA Ops:
  85.3 4.0 %copy-start = (f32[8,4,16,16]{3,2,1,0:T(8,128)S(1)}, f32[8,4,16,16]{3,2,1,0:T(8,128)}, u32[]{:S(2)}) copy-start(f32[8,4,16,16]{3,2,1,0:T(8,128)} %get-tuple-element.8) | copy-start | bytes 98308

commit v3 on v2

--- a/solution.py
+++ b/solution.py
@@ -117,6 +117,7 @@
     vel, inv, fx, fy, fz,
     out_p, out_c, out_core,
     vx, vy, vz, ip, w0, w1, w2, w3, cx, cy, cz, dinv, pp, pst, cst,
+    part, xrecv, xrecv0, xcoef, ysend, yrecv, yrecv0, yown, ycoef, yf, yd,
     zsend, zrecv, zsend0, zrecv0,
     a_send, a_recv0, a_recv1,
     wz_hi, wz_lo, fyt, k_hi, k_lo, xh, xl, u,
@@ -148,6 +149,8 @@
         pltpu.make_async_copy(vel.at[2], vz, in_sem.at[1]),
         pltpu.make_async_copy(vel.at[1], vy.at[:, pl.ds(TOP, NJ)], in_sem.at[2]),
         pltpu.make_async_copy(vel.at[0], vx.at[pl.ds(1, NI)], in_sem.at[3]),
+        pltpu.make_async_copy(inv.at[:, 0], yown.at[0], in_sem.at[4]),
+        pltpu.make_async_copy(inv.at[:, NJ - 1], yown.at[1], in_sem.at[5]),
     ]
     for c in loads:
         c.start()
@@ -158,22 +161,26 @@
 
     zero_plane = jnp.zeros((NJ, NK), F32)
     zero_row = jnp.zeros((1, NK), F32)
+    for ref in (vx, ip) + w:
+        top = 0 if ref is vx else TOP
+        for far in (0, NI + 1):
+            ref[far, pl.ds(top, NJ)] = zero_plane
+    for ref in (vy, ip) + w:
+        for i in range(NI):
+            for far in (TOP - 1, TOP + NJ):
+                ref[i if ref is vy else i + 1, pl.ds(far, 1)] = zero_row
     for s in range(2):
-        far = (0, NI + 1)[s]
-        edge = (TOP - 1, TOP + NJ)[s]
-
         @pl.when(jnp.logical_not(has[s]))
         def _():
-            vx[far] = zero_plane
-            for ref in (ip,) + w:
-                ref[far, pl.ds(TOP, NJ)] = zero_plane
+            xrecv0[s] = jnp.zeros((2, NJ, NK), F32)
+            for k in range(ITERS):
+                xrecv[k, s] = zero_plane
 
         @pl.when(jnp.logical_not(has[2 + s]))
         def _():
-            for i in range(NI):
-                vy[i, pl.ds(edge, 1)] = zero_row
-                for ref in (ip,) + w:
-                    ref[i + 1, pl.ds(edge, 1)] = zero_row
+            yrecv0[s] = jnp.zeros((2, NI, NK), F32)
+            for k in range(ITERS):
+                yrecv[k, s] = jnp.zeros((NI, NK), F32)
 
         @pl.when(jnp.logical_not(has[4 + s]))
         def _():
@@ -186,26 +193,18 @@
     def halo(r, side, landing):
         s, t = side % 2, landing % 2
         ax = side // 2
-        planes = pl.ds(1, NI)
         if ax == 0:
-            near, far = (1, NI)[s], (0, NI + 1)[t]
             if r == 0:
                 edge = (0, NI - 1)[s]
-                pairs = [
-                    (vel.at[0, edge], vx.at[far]),
-                    (inv.at[edge], ip.at[far, pl.ds(TOP, NJ)]),
-                ]
+                pairs = [(vel.at[0, edge], xrecv0.at[t, 0]), (inv.at[edge], xrecv0.at[t, 1])]
             else:
-                ref = w[r - 1]
-                pairs = [(ref.at[near, pl.ds(TOP, NJ)], ref.at[far, pl.ds(TOP, NJ)])]
+                pairs = [(w[r - 1].at[(1, NI)[s], pl.ds(TOP, NJ)], xrecv.at[r - 1, t])]
         elif ax == 1:
-            near, far = (TOP, TOP + NJ - 1)[s], (TOP - 1, TOP + NJ)[t]
             if r == 0:
                 edge = (0, NJ - 1)[s]
-                pairs = [(vel.at[1, :, edge], vy.at[:, far]), (inv.at[:, edge], ip.at[planes, far])]
+                pairs = [(vel.at[1, :, edge], yrecv0.at[t, 0]), (inv.at[:, edge], yrecv0.at[t, 1])]
             else:
-                ref = w[r - 1]
-                pairs = [(ref.at[planes, near], ref.at[planes, far])]
+                pairs = [(ysend.at[r - 1, s], yrecv.at[r - 1, t])]
         elif r == 0:
             pairs = [(zsend0, zrecv0.at[t])]
         else:
@@ -252,16 +251,29 @@
     def unpack(faces, i):
         return [pltpu.roll(faces[q % 4], lax.rem(255 - 2 * i - 64 * (q // 4), 128), 1) for q in range(8)]
 
-    def ahead(x, ends):
-        return [pltpu.roll(jnp.where(lane == 0, e, a), NK - 1, 1) for a, e in zip(x, ends)]
-
-    def behind(x, ends):
-        return [pltpu.roll(jnp.where(lane == NK - 1, e, a), 1, 1) for a, e in zip(x, ends)]
-
-    first_half = lax.broadcasted_iota(jnp.int32, (8, NK), 1) % 2 == 1
-
-    def merge(plus, minus):
-        return [jnp.where(first_half, a, b) for a, b in zip(plus, minus)]
+    odd_lane = lane % 2 == 1
+    end_lane = (lane == 0) | (lane == NK - 1)
+    sub = rows((8, NK))
+
+    def ahead(x):
+        return [jnp.where(lane == NK - 1, 0.0, pltpu.roll(a, NK - 1, 1)) for a in x]
+
+    def behind(x):
+        return [jnp.where(lane == 0, 0.0, pltpu.roll(a, 1, 1)) for a in x]
+
+    def opposite_faces(plus, minus):
+        return [
+            jnp.where(odd_lane, pltpu.roll(b, 1, 1), pltpu.roll(a, NK - 1, 1))
+            for a, b in zip(tiles(plus), tiles(minus))
+        ]
+
+    def at_ends(faces, i):
+        return [jnp.where(end_lane, e, 0.0) for e in unpack(faces, i)]
+
+    def add_rows(x, ref, i):
+        low = jnp.where(sub == 0, ref[0, pl.ds(i, 1)], 0.0)
+        high = jnp.where(sub == 7, ref[1, pl.ds(i, 1)], 0.0)
+        return [x[0] + low] + x[1:7] + [x[7] + high]
 
     GROUP = 4
     no_faces = [jnp.zeros((8, NK), F32)] * 4
@@ -314,13 +326,6 @@
 
     lax.fori_loop(0, 8, build_x, 0)
 
-    halo_wait(0, range(6))
-
-    fu = merge(tiles(zrecv0[1, 0]), tiles(zrecv0[0, 0]))
-    nminus = tiles(zrecv0[0, 1])
-    czb = [0.5 * (a + pltpu.roll(b, NK - 1, 1)) for a, b in zip(nminus, fn)]
-    fn = merge(tiles(zrecv0[1, 1]), nminus)
-
     def accumulate(acc, parts):
         while len(parts) > 1:
             parts = [parts[n] + parts[n + 1] for n in range(0, len(parts), 2)]
@@ -333,55 +338,81 @@
     def join(x):
         return jnp.concatenate(x, axis=0)
 
+    def join_edges(ref):
+        return jnp.stack([ref[1, pl.ds(TOP, NJ)], ref[NI, pl.ds(TOP, NJ)]])
+
+    cx[0] = zero_plane
+
+    def inner0(t, _):
+        for g in range(GROUP):
+            i = t * GROUP + g
+            n = ip[i + 1, pl.ds(TOP, NJ)]
+            xf = ip[i + 2, pl.ds(TOP, NJ)]
+            yn = ip[i + 1, pl.ds(TOP + 1, NJ)]
+            nt = tiles(n)
+            zn = ahead(nt)
+            cx[i + 1] = 0.5 * (n + xf)
+            cy[i, pl.ds(TOP, NJ)] = 0.5 * (n + yn)
+            cy[i, pl.ds(TOP - 1, 1)] = zero_row
+            cz[i] = join([jnp.where(lane == NK - 1, 0.0, 0.5 * (a + b)) for a, b in zip(nt, zn)])
+            around = (xf + ip[i, pl.ds(TOP, NJ)]) + (yn + ip[i + 1, pl.ds(TOP - 1, NJ)])
+            around = around + (join(zn) + join(behind(nt)))
+            dinv[i] = (SHIFT + 3.0 * n) + 0.5 * around
+            at = tiles(vz[i])
+            div = (vx[i + 2] - vx[i]) + (vy[i, pl.ds(TOP + 1, NJ)] - vy[i, pl.ds(TOP - 1, NJ)])
+            part[i] = div + (join(ahead(at)) - join(behind(at)))
+        return 0
+
+    lax.fori_loop(0, NI // GROUP, inner0, 0)
+
+    halo_wait(0, range(6))
+
+    xcoef[...] = 0.5 * (xrecv0[:, 1] + join_edges(ip))
+    ycoef[...] = 0.5 * (yrecv0[:, 1] + yown[...])
+    hn = opposite_faces(zrecv0[1, 1], zrecv0[0, 1])
+    hu = opposite_faces(zrecv0[1, 0], zrecv0[0, 0])
+    hu = [jnp.where(odd_lane, -a, a) for a in hu]
+    zcoef = [0.5 * (a + b) for a, b in zip(hn, fn)]
+    yd[...] = 0.5 * yrecv0[:, 1]
+    yf[0] = -yrecv0[0, 0]
+    yf[1] = yrecv0[1, 0]
+    hn = [0.5 * a for a in hn]
+    dinv[0] = dinv[0] + 0.5 * xrecv0[0, 1]
+    dinv[NI - 1] = dinv[NI - 1] + 0.5 * xrecv0[1, 1]
+    part[0] = part[0] - xrecv0[0, 0]
+    part[NI - 1] = part[NI - 1] + xrecv0[1, 0]
+
     def first(t, carry):
         faces, acc = carry
         terms = []
         for g in range(GROUP):
             i = t * GROUP + g
-            n = ip[i + 1, pl.ds(TOP, NJ)]
-            xf = ip[i + 2, pl.ds(TOP, NJ)]
-            yf = ip[i + 1, pl.ds(TOP + 1, NJ)]
-            xb = ip[i, pl.ds(TOP, NJ)]
-            yb = ip[i + 1, pl.ds(TOP - 1, NJ)]
-            nt = tiles(n)
-            ends = unpack(fn, i)
-            zb = join(behind(nt, ends))
-            zf = join(ahead(nt, ends))
-            cx[i + 1] = 0.5 * (n + xf)
-            cy[i, pl.ds(TOP, NJ)] = 0.5 * (n + yf)
-            cy[i, pl.ds(TOP - 1, 1)] = 0.5 * (n + yb)[0:1]
-            cz[i] = 0.5 * (n + zf)
-            d = (SHIFT + 3.0 * n) + 0.5 * (((xf + xb) + (yf + yb)) + (zf + zb))
-            at = tiles(vz[i])
-            ends = unpack(fu, i)
-            div = (vx[i + 2] - vx[i]) + (vy[i, pl.ds(TOP + 1, NJ)] - vy[i, pl.ds(TOP - 1, NJ)])
-            div = div + (join(ahead(at, ends)) - join(behind(at, ends)))
-            b = -0.5 * div
-            di = 1.0 / d
-            dinv[i] = di
-            new = b * di
-            w0[i + 1, pl.ds(TOP, NJ)] = new
-            faces = pack(faces, tiles(new), i)
-            terms += tiles(b * new)
+            row = pl.ds(i, 1)
+            d = add_rows(tiles(dinv[i]), yd, i)
+            d = [a + b for a, b in zip(d, at_ends(hn, i))]
+            b = add_rows(tiles(part[i]), yf, i)
+            b = [-0.5 * (x + y) for x, y in zip(b, at_ends(hu, i))]
+            di = [1.0 / x for x in d]
+            new = mul(b, di)
+            dinv[i] = join(di)
+            w0[i + 1, pl.ds(TOP, NJ)] = join(new)
+            ysend[0, 0, row] = new[0][0:1]
+            ysend[0, 1, row] = new[7][7:8]
+            faces = pack(faces, new, i)
+            terms += mul(b, new)
         return faces, accumulate(acc, terms)
 
-    cx[0] = 0.5 * (ip[0, pl.ds(TOP, NJ)] + ip[1, pl.ds(TOP, NJ)])
     faces, acc = lax.fori_loop(0, NI // GROUP, first, (no_faces, (zero_acc, zero_acc)))
     moments = [acc]
 
     for k in range(ITERS):
         zsend[k] = join(faces)
         halo_start(k + 1, range(6))
-        halo_wait(k + 1, range(6))
-        after = tiles(zrecv[k, 1])
-        flux = merge(after, mul(czb, tiles(zrecv[k, 0])))
         last = k == ITERS - 1
         here = w[k]
-        there = None if last else w[k + 1]
-
-        def step(t, carry):
-            faces, odd, even = carry
-            t_odd, t_even = [], []
+
+        def inner(t, odd):
+            terms = []
             for g in range(GROUP):
                 i = t * GROUP + g
                 c = here[i + 1, pl.ds(TOP, NJ)]
@@ -389,24 +420,52 @@
                 bw = cx[i] * here[i, pl.ds(TOP, NJ)] + cx[i + 1] * here[i + 2, pl.ds(TOP, NJ)]
                 bw = bw + cy[i, pl.ds(TOP - 1, NJ)] * here[i + 1, pl.ds(TOP - 1, NJ)]
                 bw = bw + cy[i, pl.ds(TOP, NJ)] * here[i + 1, pl.ds(TOP + 1, NJ)]
-                ends = unpack(flux, i)
-                bw = bw + (f * join(ahead(tiles(c), ends)) + join(behind(tiles(f * c), ends)))
-                t_odd += tiles(c * bw)
-                if not last:
-                    new = bw * dinv[i]
-                    t_even += tiles(bw * new)
-                    there[i + 1, pl.ds(TOP, NJ)] = new
-                    faces = pack(faces, tiles(new), i)
-            odd = accumulate(odd, t_odd)
+                nxt = join([pltpu.roll(a, NK - 1, 1) for a in tiles(c)])
+                prv = join([pltpu.roll(a, 1, 1) for a in tiles(f * c)])
+                bw = bw + (f * nxt + prv)
+                part[i] = bw
+                terms += tiles(c * bw)
+            return accumulate(odd, terms)
+
+        odd = lax.fori_loop(0, NI // GROUP, inner, (zero_acc, zero_acc))
+
+        halo_wait(k + 1, range(6))
+        flux = mul(zcoef, opposite_faces(zrecv[k, 1], zrecv[k, 0]))
+        terms = mul(flux, faces)
+        for s in range(2):
+            side = ycoef[s] * yrecv[k, s]
+            yf[s] = side
+            terms += tiles(side * ysend[k, s])
+            side = xcoef[s] * xrecv[k, s]
+            edge = (0, NI - 1)[s]
+            terms += tiles(side * here[edge + 1, pl.ds(TOP, NJ)])
             if not last:
-                even = accumulate(even, t_even)
-            return faces, odd, even
-
-        start = (no_faces, (zero_acc, zero_acc), (zero_acc, zero_acc))
-        faces, odd, even = lax.fori_loop(0, NI // GROUP, step, start)
-        moments.append(odd)
-        if not last:
-            moments.append(even)
+                part[edge] = part[edge] + side
+        while len(terms) & (len(terms) - 1):
+            terms.append(zero_acc)
+        moments.append(accumulate(odd, terms))
+        if last:
+            break
+        there = w[k + 1]
+
+        def outer(t, carry):
+            faces, even = carry
+            terms = []
+            for g in range(GROUP):
+                i = t * GROUP + g
+                row = pl.ds(i, 1)
+                bw = add_rows(tiles(part[i]), yf, i)
+                bw = [a + b for a, b in zip(bw, at_ends(flux, i))]
+                new = mul(bw, tiles(dinv[i]))
+                there[i + 1, pl.ds(TOP, NJ)] = join(new)
+                ysend[k + 1, 0, row] = new[0][0:1]
+                ysend[k + 1, 1, row] = new[7][7:8]
+                faces = pack(faces, new, i)
+                terms += mul(bw, new)
+            return faces, accumulate(even, terms)
+
+        faces, even = lax.fori_loop(0, NI // GROUP, outer, (no_faces, (zero_acc, zero_acc)))
+        moments.append(even)
 
     row8 = rows((8, NK))
     lane8 = lanes((8, NK))
@@ -456,10 +515,12 @@
             total = total + c * x
         return total
 
-    pe = combine([join(merge(tiles(zrecv[k, 1]), tiles(zrecv[k, 0]))) for k in range(ITERS)])
-    pe = tiles(pe)
-    for far in (0, NI + 1):
-        pp[far, pl.ds(TOP, NJ)] = combine([ref[far, pl.ds(TOP, NJ)] for ref in w])
+    pe = [opposite_faces(zrecv[k, 1], zrecv[k, 0]) for k in range(ITERS)]
+    pe = [combine(list(parts)) for parts in zip(*pe)]
+    pe = [jnp.where(odd_lane, -a, a) for a in pe]
+    for s in range(2):
+        pp[(0, NI + 1)[s], pl.ds(TOP, NJ)] = combine([xrecv[k, s] for k in range(ITERS)])
+        yf[s] = combine([yrecv[k, s] for k in range(ITERS)])
 
     def keep(f, i, x):
         hi, lo = split(x)
@@ -471,8 +532,8 @@
     def press(t, _):
         for g in range(GROUP):
             i = t * GROUP + g
-            for top, n in ((TOP - 1, 1), (TOP + NJ, 1)):
-                pp[i + 1, pl.ds(top, n)] = combine([ref[i + 1, pl.ds(top, n)] for ref in w])
+            pp[i + 1, pl.ds(TOP - 1, 1)] = yf[0, pl.ds(i, 1)]
+            pp[i + 1, pl.ds(TOP + NJ, 1)] = yf[1, pl.ds(i, 1)]
             x = combine([ref[i + 1, pl.ds(TOP, NJ)] for ref in w])
             pp[i + 1, pl.ds(TOP, NJ)] = x
             pst[i] = x
@@ -494,8 +555,7 @@
                     x = vy[i, pl.ds(TOP, NJ)]
                 else:
                     c = tiles(pp[i + 1, pl.ds(TOP, NJ)])
-                    ends = unpack(pe, i)
-                    g_ = join(ahead(c, ends)) - join(behind(c, ends))
+                    g_ = join(ahead(c)) - join(behind(c)) + join(at_ends(pe, i))
                     x = vz[i]
                 x = x - n * (0.5 * g_)
                 cst[f, i] = x
@@ -650,6 +710,17 @@
         pltpu.VMEM((NI + 2, tall, NK), F32),
         pltpu.VMEM((NI, NJ, NK), F32),
         pltpu.VMEM((3, NI, NJ, NK), F32),
+        pltpu.VMEM((NI, NJ, NK), F32),
+        pltpu.VMEM((ITERS, 2, NJ, NK), F32),
+        pltpu.VMEM((2, 2, NJ, NK), F32),
+        pltpu.VMEM((2, NJ, NK), F32),
+        pltpu.VMEM((ITERS, 2, NI, NK), F32),
+        pltpu.VMEM((ITERS, 2, NI, NK), F32),
+        pltpu.VMEM((2, 2, NI, NK), F32),
+        pltpu.VMEM((2, NI, NK), F32),
+        pltpu.VMEM((2, NI, NK), F32),
+        pltpu.VMEM((2, NI, NK), F32),
+        pltpu.VMEM((2, NI, NK), F32),
         pltpu.VMEM((ITERS, 32, NK), F32),
         pltpu.VMEM((ITERS, 2, 32, NK), F32),
         pltpu.VMEM((2, 32, NK), F32),
@@ -674,7 +745,7 @@
         pltpu.VMEM((64, 512), F32),
         pltpu.VMEM((8, 64, 128), F32),
         pltpu.VMEM((7, 64, 128), F32),
-        dma((4,)),
+        dma((6,)),
         dma((4,)),
         dma((5, 6, 2)),
         dma((5, 6, 2)),

time: 90.2 us -> 85.3 us (0.946)
  Pallas kernels: 82.4 us -> 77.4 us
    pallas_call x1, Pallas kernels: 82.4 us -> 77.4 us  [per_device(): pl.pallas_call(kernel, out_shape=(jax.ShapeDtypeStruct(inv_density.shape,...]
where the time goes in v3:
time: 85.3 us; the launch traced here: 85.1 us
  Pallas kernels  77.4 us (91%)
  local copies, waits for them, and re-layouts  7.02 us (8%)
    pallas_call x1, Pallas kernels, per_device(): pl.pallas_call(kernel, out_shape=(jax.ShapeDtypeStruct(inv_density.shape,...  77.4 us
    unnamed x5, local copies, waits for them, and re-layouts  7.02 us

profile of v3, /device:TPU:1, one launch (start us, length us, event | category | flops | bytes accessed | tf_op | source)
XLA Modules:
  0.0 85.1 jit_solution(3938757173995359334)
XLA Ops:
  0.6 77.4 %shard_map.76 = (f32[32,64,128]{2,1,0:T(8,128)}, f32[3,32,64,128]{3,2,1,0:T(8,128)}, f32[8,4,16,16]{3,2,1,0:T(8,128)}) custom-call(f32[3,32,64,128]{3,2,1,0:T(8,128)} %vel.1, f32[32,64,128]{2,1,0:T(8,128)} %inv.1, f32[32,64]{1,0:T(8,128)} %fx.1, f32[64,64]{1,0:T(8,128)} %fy.1, f32[64,128]{1,0:T(8,128)} %bitcast.1), custom_call_target="tpu_custom_call" | custom-call | tf_op jit(solution)/shard_map/pallas_call | solution.py:759
  78.1 2.3 %copy.11 = f32[32,64,128]{2,1,0:T(8,128)} copy(f32[32,64,128]{2,1,0:T(8,128)} %get-tuple-element.6) | data formatting | bytes 2097152
  80.4 0.0 copy-start
  80.4 4.0 %copy.12 = f32[3,32,64,128]{3,2,1,0:T(8,128)} copy(f32[3,32,64,128]{3,2,1,0:T(8,128)} %get-tuple-element.7) | data formatting | bytes 6291456
  84.4 0.0 copy-done
  84.4 0.7 copy.13
Async XLA Ops:
  80.4 4.0 %copy-start = (f32[8,4,16,16]{3,2,1,0:T(8,128)S(1)}, f32[8,4,16,16]{3,2,1,0:T(8,128)}, u32[]{:S(2)}) copy-start(f32[8,4,16,16]{3,2,1,0:T(8,128)} %get-tuple-element.8) | copy-start | bytes 98308

commit v4 on v3

--- a/solution.py
+++ b/solution.py
@@ -34,6 +34,15 @@
 def df_add(x, y):
     s, e = two_sum(x[0], y[0])
     return quick(s, e + (x[1] + y[1]))
+
+
+def exact_sum(x):
+    def total(a):
+        return jnp.sum(jnp.sum(a, axis=0, keepdims=True), axis=1, keepdims=True)
+
+    big = 4.0 * total(jnp.abs(x[0]))
+    coarse = (x[0] + big) - big
+    return quick(total(coarse), total((x[0] - coarse) + x[1]))
 
 
 def df_neg(x):
@@ -115,15 +124,15 @@
 
 def kernel(
     vel, inv, fx, fy, fz,
-    out_p, out_c, out_core,
-    vx, vy, vz, ip, w0, w1, w2, w3, cx, cy, cz, dinv, pp, pst, cst,
+    pst, cst, out_core,
+    vx, vy, vz, ip, w0, w1, w2, w3, cx, cy, cz, dinv, pp,
     part, xrecv, xrecv0, xcoef, ysend, yrecv, yrecv0, yown, ycoef, yf, yd,
     zsend, zrecv, zsend0, zrecv0,
     a_send, a_recv0, a_recv1,
-    wz_hi, wz_lo, fyt, k_hi, k_lo, xh, xl, u,
+    wz, fyt, k_hi, k_lo, xh, xl, u,
     za_in, za_acc, za_dir, za_out, ya_in, ya_acc, ya_dir, ya_out,
     b_src_z, b_src_y, b_in, b_acc, b_dir, b_out, ysc, v, v_recv,
-    in_sem, out_sem, hs_sem, hr_sem, as_sem, ar_sem, rs_sem, rr_sem, xs_sem, xr_sem,
+    in_sem, hs_sem, hr_sem, as_sem, ar_sem, rs_sem, rr_sem, xs_sem, xr_sem,
 ):
     w = (w0, w1, w2, w3)
     me = [lax.axis_index(a) for a in AXES]
@@ -158,6 +167,47 @@
     barrier = pltpu.get_barrier_semaphore()
     for side in range(6):
         pl.semaphore_signal(barrier, inc=1, device_id=neighbour(side), device_id_type=MESH)
+
+    def tiles(x):
+        return [x[8 * q : 8 * q + 8] for q in range(x.shape[0] // 8)]
+
+    def pack(acc, x, i):
+        out = list(acc)
+        for q, part in enumerate(x):
+            moved = pltpu.roll(part, 2 * i + 1 + 64 * (q // 4), 1)
+            out[q % 4] = jnp.where(lane // 2 == i + 32 * (q // 4), moved, out[q % 4])
+        return out
+
+    def unpack(faces, i):
+        return [pltpu.roll(faces[q % 4], lax.rem(255 - 2 * i - 64 * (q // 4), 128), 1) for q in range(8)]
+
+    odd_lane = lane % 2 == 1
+    end_lane = (lane == 0) | (lane == NK - 1)
+    sub = rows((8, NK))
+
+    def ahead(x):
+        return [jnp.where(lane == NK - 1, 0.0, pltpu.roll(a, NK - 1, 1)) for a in x]
+
+    def behind(x):
+        return [jnp.where(lane == 0, 0.0, pltpu.roll(a, 1, 1)) for a in x]
+
+    def opposite_faces(plus, minus):
+        return [
+            jnp.where(odd_lane, pltpu.roll(b, 1, 1), pltpu.roll(a, NK - 1, 1))
+            for a, b in zip(tiles(plus), tiles(minus))
+        ]
+
+    def at_ends(faces, i):
+        return [jnp.where(end_lane, e, 0.0) for e in unpack(faces, i)]
+
+    def add_rows(x, ref, i):
+        low = jnp.where(sub == 0, ref[0, pl.ds(i, 1)], 0.0)
+        high = jnp.where(sub == 7, ref[1, pl.ds(i, 1)], 0.0)
+        return [x[0] + low] + x[1:7] + [x[7] + high]
+
+    GROUP = 4
+    no_faces = [jnp.zeros((8, NK), F32)] * 4
+    zero_acc = jnp.zeros((8, NK), F32)
 
     zero_plane = jnp.zeros((NJ, NK), F32)
     zero_row = jnp.zeros((1, NK), F32)
@@ -188,6 +238,20 @@
             for k in range(ITERS):
                 zrecv[k, s] = jnp.zeros((32, NK), F32)
 
+    for c in loads[:2]:
+        c.wait()
+
+    def face0(t, carry):
+        a, b = carry
+        for g in range(GROUP):
+            i = t * GROUP + g
+            a = pack(a, tiles(vz[i]), i)
+            b = pack(b, tiles(ip[i + 1, pl.ds(TOP, NJ)]), i)
+        return a, b
+
+    fu, fn = lax.fori_loop(0, NI // GROUP, face0, (no_faces, no_faces))
+    zsend0[0] = jnp.concatenate(fu, axis=0)
+    zsend0[1] = jnp.concatenate(fn, axis=0)
     pl.semaphore_wait(barrier, 6)
 
     def halo(r, side, landing):
@@ -236,95 +300,10 @@
                 for c in halo(r, side, side ^ 1):
                     c.wait_send()
 
-    halo_start(0, range(4))
-
-    def tiles(x):
-        return [x[8 * q : 8 * q + 8] for q in range(x.shape[0] // 8)]
-
-    def pack(acc, x, i):
-        out = list(acc)
-        for q, part in enumerate(x):
-            moved = pltpu.roll(part, 2 * i + 1 + 64 * (q // 4), 1)
-            out[q % 4] = jnp.where(lane // 2 == i + 32 * (q // 4), moved, out[q % 4])
-        return out
-
-    def unpack(faces, i):
-        return [pltpu.roll(faces[q % 4], lax.rem(255 - 2 * i - 64 * (q // 4), 128), 1) for q in range(8)]
-
-    odd_lane = lane % 2 == 1
-    end_lane = (lane == 0) | (lane == NK - 1)
-    sub = rows((8, NK))
-
-    def ahead(x):
-        return [jnp.where(lane == NK - 1, 0.0, pltpu.roll(a, NK - 1, 1)) for a in x]
-
-    def behind(x):
-        return [jnp.where(lane == 0, 0.0, pltpu.roll(a, 1, 1)) for a in x]
-
-    def opposite_faces(plus, minus):
-        return [
-            jnp.where(odd_lane, pltpu.roll(b, 1, 1), pltpu.roll(a, NK - 1, 1))
-            for a, b in zip(tiles(plus), tiles(minus))
-        ]
-
-    def at_ends(faces, i):
-        return [jnp.where(end_lane, e, 0.0) for e in unpack(faces, i)]
-
-    def add_rows(x, ref, i):
-        low = jnp.where(sub == 0, ref[0, pl.ds(i, 1)], 0.0)
-        high = jnp.where(sub == 7, ref[1, pl.ds(i, 1)], 0.0)
-        return [x[0] + low] + x[1:7] + [x[7] + high]
-
-    GROUP = 4
-    no_faces = [jnp.zeros((8, NK), F32)] * 4
-    zero_acc = jnp.zeros((8, NK), F32)
-
-    for c in loads[:2]:
-        c.wait()
-
-    def face0(t, carry):
-        a, b = carry
-        for g in range(GROUP):
-            i = t * GROUP + g
-            a = pack(a, tiles(vz[i]), i)
-            b = pack(b, tiles(ip[i + 1, pl.ds(TOP, NJ)]), i)
-        return a, b
-
-    fu, fn = lax.fori_loop(0, NI // GROUP, face0, (no_faces, no_faces))
-    zsend0[0] = jnp.concatenate(fu, axis=0)
-    zsend0[1] = jnp.concatenate(fn, axis=0)
-    halo_start(0, (4, 5))
+    halo_start(0, range(6))
+
     for c in loads[2:]:
         c.wait()
-
-    fzp = jnp.concatenate([fz[...], jnp.zeros((64, NK), F32)], axis=0).T
-    lane_k = lanes((NK, 128))
-
-    def build_z(i8, _):
-        row = pl.ds(pl.multiple_of(i8 * 128, 128), 128)
-        for r in range(4):
-            moved = pltpu.roll(fzp, lax.rem(16 * i8 + 128 - 16 * r, 128), 1)
-            hi, lo = split(jnp.where(lane_k // 16 == i8, moved, 0.0))
-            wz_hi[row, pl.ds(128 * r, 128)] = hi
-            wz_lo[row, pl.ds(128 * r, 128)] = lo
-        return 0
-
-    lax.fori_loop(0, 8, build_z, 0)
-    fyp = jnp.concatenate([fy[...], jnp.zeros((NJ, 64), F32)], axis=1)
-    hi, lo = split(fyp.T[:64])
-    fyt[...] = jnp.concatenate([hi, lo, hi], axis=1)
-    fx_hi, fx_lo = split(fx[...])
-    rep = (rows((512, NI)) // 16 == lanes((512, NI))).astype(F32).astype(BF16)
-    same = (rows((512, 128)) % 16) == (lanes((512, 128)) % 16)
-
-    def build_x(m, _):
-        pick = (rows((64, 128)) == 8 * m + lanes((64, 128)) // 16).astype(F32).astype(BF16)
-        for part, dst in ((fx_hi, k_hi), (fx_lo, k_lo)):
-            wide = dot(part, pick).astype(BF16)
-            dst[m] = jnp.where(same, dot(rep, wide), 0.0).astype(BF16)
-        return 0
-
-    lax.fori_loop(0, 8, build_x, 0)
 
     def accumulate(acc, parts):
         while len(parts) > 1:
@@ -467,18 +446,37 @@
         faces, even = lax.fori_loop(0, NI // GROUP, outer, (no_faces, (zero_acc, zero_acc)))
         moments.append(even)
 
+    def build_operands():
+        fzp = jnp.concatenate([fz[...], jnp.zeros((64, NK), F32)], axis=0).T
+        hi, lo = split(jnp.concatenate([fzp, pltpu.roll(fzp, 64, 1)], axis=0))
+        wz[...] = jnp.concatenate([hi, lo], axis=1)
+        fyp = jnp.concatenate([fy[...], jnp.zeros((NJ, 64), F32)], axis=1)
+        hi, lo = split(fyp.T[:64])
+        fyt[...] = jnp.concatenate([hi, lo, hi], axis=1)
+        fx_hi, fx_lo = split(fx[...])
+        row = rows((512, NI))
+        plane = (row // 128) * 8 + ((row % 64) // 16) * 2 + (row % 128) // 64
+        rep = (plane == lanes((512, NI))).astype(F32).astype(BF16)
+        same = (rows((512, 128)) % 16) == (lanes((512, 128)) % 16)
+
+        def build_x(m, _):
+            pick = (rows((64, 128)) == 8 * m + lanes((64, 128)) // 16).astype(F32).astype(BF16)
+            for part_, dst in ((fx_hi, k_hi), (fx_lo, k_lo)):
+                wide = dot(part_, pick).astype(BF16)
+                dst[m] = jnp.where(same, dot(rep, wide), 0.0).astype(BF16)
+            return 0
+
+        lax.fori_loop(0, 8, build_x, 0)
+
     row8 = rows((8, NK))
     lane8 = lanes((8, NK))
     hi = zero_acc
     lo = zero_acc
     for m, acc in enumerate(moments):
-        for shift in (4, 2, 1):
-            acc = df_add(acc, (pltpu.roll(acc[0], shift, 0), pltpu.roll(acc[1], shift, 0)))
+        acc = exact_sum(acc)
         hi = jnp.where(row8 == m, acc[0], hi)
         lo = jnp.where(row8 == m, acc[1], lo)
     total = (hi, lo)
-    for shift in (64, 32, 16, 8, 4, 2, 1):
-        total = df_add(total, (pltpu.roll(total[0], shift, 1), pltpu.roll(total[1], shift, 1)))
 
     plane_to = [{"gy": lax.rem(me[1] + dy, 4), "gz": lax.rem(me[2] + dz, 4)} for dy, dz in PLANE]
     line_to = [{"gx": lax.rem(me[0] + o, 8)} for o in range(1, 8)]
@@ -490,6 +488,8 @@
         ]
         for c in copies:
             c.start()
+        if stage == 0:
+            build_operands()
         for c in copies:
             c.wait_recv()
         terms = [total]
@@ -522,10 +522,10 @@
         pp[(0, NI + 1)[s], pl.ds(TOP, NJ)] = combine([xrecv[k, s] for k in range(ITERS)])
         yf[s] = combine([yrecv[k, s] for k in range(ITERS)])
 
-    def keep(f, i, x):
+    def keep(f, i, x, odd_plane):
         hi, lo = split(x)
-        rr = pl.ds(pl.multiple_of((i // 8) * NJ, NJ), NJ)
-        cc = pl.ds(pl.multiple_of(lax.rem(i, 8) * NK, NK), NK)
+        rr = pl.ds(pl.multiple_of((i // 2) * NJ, NJ), NJ)
+        cc = slice(NK * odd_plane, NK * odd_plane + NK)
         xh[f, rr, cc] = hi
         xl[f, rr, cc] = lo
 
@@ -537,7 +537,7 @@
             x = combine([ref[i + 1, pl.ds(TOP, NJ)] for ref in w])
             pp[i + 1, pl.ds(TOP, NJ)] = x
             pst[i] = x
-            keep(3, i, x)
+            keep(3, i, x, g % 2)
         return 0
 
     lax.fori_loop(0, NI // GROUP, press, 0)
@@ -559,7 +559,7 @@
                     x = vz[i]
                 x = x - n * (0.5 * g_)
                 cst[f, i] = x
-                keep(f, i, x)
+                keep(f, i, x, g % 2)
             return 0
 
         lax.fori_loop(0, NI // GROUP, body, 0)
@@ -622,27 +622,34 @@
         relay.wait_recv()
         return chunk(me[AXES.index(axis)])[...] + r_acc[...] + r_dir[...]
 
+    block = (lane % 64) // 16
+
     def contract(f):
-        wh, wl = wz_hi[...], wz_lo[...]
-        a, b = xh[f], xl[f]
-        for half in range(2):
-            cols = slice(256 * half, 256 * half + 256)
-            z = dot(a, wh[:, cols]) + dot(b, wh[:, cols]) + dot(a, wl[:, cols])
-            for g in range(4):
-                hi, lo = split(z[NJ * g : NJ * g + NJ])
+        operand = wz[...]
+        for g in range(4):
+            cut = slice(256 * g, 256 * g + 256)
+            both = dot(xh[f, cut], operand)
+            z = (both[:, :128] + both[:, 128:]) + dot(xl[f, cut], operand[:, :128])
+            done = []
+            for h in range(2):
+                pair = [z[NJ * n : NJ * n + NJ] for n in (2 * h, 2 * h + 1)]
+                hi, lo = split(jnp.concatenate(pair, axis=1))
                 y = dot(fyt[...], jnp.concatenate([hi, hi, lo], axis=0))
-                u[f, 2 * half, g] = y[:, :128]
-                u[f, 2 * half + 1, g] = y[:, 128:]
-
-    stores = [pltpu.make_async_copy(pst, out_p, out_sem.at[3])]
-    stores[0].start()
-    pending.append(stores[0].wait)
+                done += [tiles(y[:, :128]), tiles(y[:, 128:])]
+            for r in range(4):
+                out = []
+                for q in range(8):
+                    acc = done[r][q]
+                    for n in range(4):
+                        if n != r:
+                            moved = pltpu.roll(done[n][q], (16 * (n - r)) % 128, 1)
+                            acc = jnp.where(block == n, moved, acc)
+                    out.append(acc)
+                u[f, r, g] = join(out)
+
     for f in ORDER:
         if f != 3:
             fix(f)
-            stores.append(pltpu.make_async_copy(cst.at[f], out_c.at[f], out_sem.at[f]))
-            stores[-1].start()
-            pending.append(stores[-1].wait)
         contract(f)
         stage_open(f, 0)
     for f in ORDER:
@@ -709,8 +716,6 @@
         pltpu.VMEM((NI, NJ, NK), F32),
         pltpu.VMEM((NI + 2, tall, NK), F32),
         pltpu.VMEM((NI, NJ, NK), F32),
-        pltpu.VMEM((3, NI, NJ, NK), F32),
-        pltpu.VMEM((NI, NJ, NK), F32),
         pltpu.VMEM((ITERS, 2, NJ, NK), F32),
         pltpu.VMEM((2, 2, NJ, NK), F32),
         pltpu.VMEM((2, NJ, NK), F32),
@@ -728,13 +733,12 @@
         pltpu.VMEM((2, 8, NK), F32),
         pltpu.VMEM((len(PLANE), 8, NK), F32),
         pltpu.VMEM((7, 8, NK), F32),
-        pltpu.VMEM((1024, 512), BF16),
-        pltpu.VMEM((1024, 512), BF16),
+        pltpu.VMEM((256, 256), BF16),
         pltpu.VMEM((64, 192), BF16),
         pltpu.VMEM((8, 512, 128), BF16),
         pltpu.VMEM((8, 512, 128), BF16),
-        pltpu.VMEM((4, 256, 1024), BF16),
-        pltpu.VMEM((4, 256, 1024), BF16),
+        pltpu.VMEM((4, 1024, 256), BF16),
+        pltpu.VMEM((4, 1024, 256), BF16),
         pltpu.VMEM((4, 4, 4, 64, 128), F32),
     ]
     scratch += [pltpu.VMEM((2, 4, 64, 128), F32)] * 4
@@ -746,7 +750,6 @@
         pltpu.VMEM((8, 64, 128), F32),
         pltpu.VMEM((7, 64, 128), F32),
         dma((6,)),
-        dma((4,)),
         dma((5, 6, 2)),
         dma((5, 6, 2)),
         dma((2, len(PLANE))),
@@ -756,20 +759,21 @@
         dma((7,)),
         dma((7,)),
     ]
-    return pl.pallas_call(
+    pressure, corrected, core = pl.pallas_call(
         kernel,
         out_shape=(
-            jax.ShapeDtypeStruct(inv_density.shape, F32),
-            jax.ShapeDtypeStruct(velocity.shape, F32),
-            jax.ShapeDtypeStruct((8, 4, 16, 16), F32),
+            pltpu.VMEM(inv_density.shape, F32),
+            pltpu.VMEM(velocity.shape, F32),
+            pltpu.VMEM((8, 4, 16, 16), F32),
         ),
         in_specs=[hbm, hbm, vmem, vmem, vmem],
-        out_specs=(hbm, hbm, vmem),
+        out_specs=(vmem, vmem, vmem),
         scratch_shapes=scratch,
         compiler_params=pltpu.CompilerParams(
-            collective_id=0, has_side_effects=True, vmem_limit_bytes=60 * 1024 * 1024
+            collective_id=0, has_side_effects=True, vmem_limit_bytes=52 * 1024 * 1024
         ),
     )(velocity, inv_density, factor_x, factor_y, factor_z.T)
+    return pressure, corrected, core
 
 
 def solution(mesh):

time: 85.3 us -> 74.1 us (0.87)
  Pallas kernels: 77.4 us -> 69.9 us
  local copies, waits for them, and re-layouts: 7.02 us -> 3.34 us
    pallas_call x1, Pallas kernels: 77.4 us -> 69.9 us  [per_device(): pl.pallas_call(kernel, out_shape=(pltpu.VMEM(inv_density.shape, F32), plt...]
    unnamed x5 -> x3, local copies, waits for them, and re-layouts: 7.02 us -> 3.34 us
where the time goes in v4:
time: 74.1 us; the launch traced here: 73.9 us
  Pallas kernels  69.9 us (94%)
  local copies, waits for them, and re-layouts  3.34 us (5%)
    pallas_call x1, Pallas kernels, per_device(): pl.pallas_call(kernel, out_shape=(pltpu.VMEM(inv_density.shape, F32), plt...  69.9 us
    unnamed x3, local copies, waits for them, and re-layouts  3.34 us

profile of v4, /device:TPU:1, one launch (start us, length us, event | category | flops | bytes accessed | tf_op | source)
XLA Modules:
  0.0 73.9 jit_solution(7087697235957484063)
XLA Ops:
  0.6 69.9 %shard_map.76 = (f32[32,64,128]{2,1,0:T(8,128)S(1)}, f32[3,32,64,128]{3,2,1,0:T(8,128)S(1)}, f32[8,4,16,16]{3,2,1,0:T(8,128)S(1)}) custom-call(f32[3,32,64,128]{3,2,1,0:T(8,128)} %vel.1, f32[32,64,128]{2,1,0:T(8,128)} %inv.1, f32[32,64]{1,0:T(8,128)} %fx.1, f32[64,64]{1,0:T(8,128)} %fy.1, f32[64,128]{1,0:T(8,128)} %bitcast.1), custom_call_target="tpu_custom_call" | custom-call | tf_op jit(solution)/shard_map/pallas_call | solution.py:762
  70.6 1.0 %copy.11 = f32[32,64,128]{2,1,0:T(8,128)} copy(f32[32,64,128]{2,1,0:T(8,128)S(1)} %get-tuple-element.3) | data formatting | bytes 2097152
  71.5 0.7 copy.13
  72.2 1.7 %copy.12 = f32[3,32,64,128]{3,2,1,0:T(8,128)} copy(f32[3,32,64,128]{3,2,1,0:T(8,128)S(1)} %get-tuple-element.4) | data formatting | bytes 6291456

commit v5 on v4

--- a/solution.py
+++ b/solution.py
@@ -129,7 +129,7 @@
     part, xrecv, xrecv0, xcoef, ysend, yrecv, yrecv0, yown, ycoef, yf, yd,
     zsend, zrecv, zsend0, zrecv0,
     a_send, a_recv0, a_recv1,
-    wz, fyt, k_hi, k_lo, xh, xl, u,
+    wz, zb, fyt, k_hi, k_lo, xh, xl, u,
     za_in, za_acc, za_dir, za_out, ya_in, ya_acc, ya_dir, ya_out,
     b_src_z, b_src_y, b_in, b_acc, b_dir, b_out, ysc, v, v_recv,
     in_sem, hs_sem, hr_sem, as_sem, ar_sem, rs_sem, rr_sem, xs_sem, xr_sem,
@@ -447,15 +447,20 @@
         moments.append(even)
 
     def build_operands():
-        fzp = jnp.concatenate([fz[...], jnp.zeros((64, NK), F32)], axis=0).T
-        hi, lo = split(jnp.concatenate([fzp, pltpu.roll(fzp, 64, 1)], axis=0))
-        wz[...] = jnp.concatenate([hi, lo], axis=1)
+        twice = jnp.concatenate([fz[...], fz[...]], axis=0).T
+        low_half = lanes((NK, 128)) < 64
+        for n in range(4):
+            turned = twice if n == 0 else pltpu.roll(twice, 16 * n, 1)
+            top = jnp.where(low_half, turned, 0.0)
+            hi, lo = split(jnp.concatenate([top, turned - top], axis=0))
+            wz[n] = jnp.concatenate([hi, lo], axis=1)
         fyp = jnp.concatenate([fy[...], jnp.zeros((NJ, 64), F32)], axis=1)
         hi, lo = split(fyp.T[:64])
         fyt[...] = jnp.concatenate([hi, lo, hi], axis=1)
         fx_hi, fx_lo = split(fx[...])
         row = rows((512, NI))
-        plane = (row // 128) * 8 + ((row % 64) // 16) * 2 + (row % 128) // 64
+        pair = ((row % 64) // 16 + 4 - me[2]) % 4
+        plane = (row // 128) * 8 + pair * 2 + (row % 128) // 64
         rep = (plane == lanes((512, NI))).astype(F32).astype(BF16)
         same = (rows((512, 128)) % 16) == (lanes((512, 128)) % 16)
 
@@ -503,8 +508,7 @@
                 for t in range(0, len(terms), 2)
             ]
         total = terms[0]
-        for c in copies:
-            c.wait_send()
+        pending.extend(c.wait_send for c in copies)
 
     nu = [(total[0][m : m + 1], total[1][m : m + 1]) for m in range(2 * ITERS)]
     coef = solve4(nu)
@@ -524,7 +528,7 @@
 
     def keep(f, i, x, odd_plane):
         hi, lo = split(x)
-        rr = pl.ds(pl.multiple_of((i // 2) * NJ, NJ), NJ)
+        rr = pl.ds(pl.multiple_of((lax.rem(i // 2, 4) * 4 + i // 8) * NJ, NJ), NJ)
         cc = slice(NK * odd_plane, NK * odd_plane + NK)
         xh[f, rr, cc] = hi
         xl[f, rr, cc] = lo
@@ -575,117 +579,128 @@
     def rows16(m):
         return pl.ds(pl.multiple_of(m * 16, 16), 16)
 
-    def stage_refs(f, stage):
+    def stage_refs(f, h, stage):
         axis, way = ROUTES[f]
         slot = 0 if way == 1 else 1
+        part_ = pl.ds(2 * h, 2)
         if stage == 0:
             if axis == "gz":
-                return axis, way, (lambda m: u.at[f, m]), za_in.at[slot], za_acc.at[slot], za_dir.at[slot], za_out.at[slot]
-            return axis, way, (lambda m: u.at[f, :, :, rows16(m)]), ya_in.at[slot], ya_acc.at[slot], ya_dir.at[slot], ya_out.at[slot]
+                return axis, way, (lambda m: u.at[f, m, part_]), za_in.at[slot, h], za_acc.at[slot, h], za_dir.at[slot, h], za_out.at[slot, h]
+            return axis, way, (lambda m: u.at[f, :, part_, rows16(m)]), ya_in.at[slot, h], ya_acc.at[slot, h], ya_dir.at[slot, h], ya_out.at[slot, h]
         other = "gy" if axis == "gz" else "gz"
         if axis == "gz":
-            chunk = lambda m: b_src_z.at[slot, :, rows16(m)]
+            chunk = lambda m: b_src_z.at[slot, h, :, rows16(m)]
         else:
-            chunk = lambda m: b_src_y.at[slot, m]
-        return other, way, chunk, b_in.at[f], b_acc.at[f], b_dir.at[f], b_out.at[f]
-
-    def stage_copies(f, stage):
-        axis, way, chunk, r_in, r_acc, r_dir, r_out = stage_refs(f, stage)
+            chunk = lambda m: b_src_y.at[slot, h, m]
+        return other, way, chunk, b_in.at[f, h], b_acc.at[f, h], b_dir.at[f, h], b_out.at[f, h]
+
+    def stage_far(f, h, stage):
+        axis, way, chunk, r_in, r_acc, r_dir, r_out = stage_refs(f, h, stage)
         to, back, opposite = ring(axis, way)
-        sems = lambda n: (rs_sem.at[f, stage, n], rr_sem.at[f, stage, n])
-        return (
-            remote(chunk(opposite), r_in, *sems(0), {axis: to}),
-            remote(chunk(back), r_dir, *sems(1), {axis: back}),
-            remote(r_out, r_acc, *sems(2), {axis: to}),
-        )
-
-    def stage_open(f, stage):
-        far, near, _ = stage_copies(f, stage)
-        far.start()
-        near.start()
-        pending.append(far.wait_send)
-        pending.append(near.wait_send)
-
-    def stage_relay(f, stage):
-        axis, way, chunk, r_in, r_acc, r_dir, r_out = stage_refs(f, stage)
+        return remote(chunk(opposite), r_in, rs_sem.at[f, h, stage, 0], rr_sem.at[f, h, stage, 0], {axis: to})
+
+    def stage_near(f, h, stage):
+        axis, way, chunk, r_in, r_acc, r_dir, r_out = stage_refs(f, h, stage)
         to, back, opposite = ring(axis, way)
-        far, near, relay = stage_copies(f, stage)
-        far.wait_recv()
-        r_out[...] = r_in[...] + chunk(to)[...]
+        return remote(chunk(back), r_dir, rs_sem.at[f, h, stage, 1], rr_sem.at[f, h, stage, 1], {axis: back})
+
+    def stage_next(f, h, stage):
+        axis, way, chunk, r_in, r_acc, r_dir, r_out = stage_refs(f, h, stage)
+        to, back, opposite = ring(axis, way)
+        return remote(r_out, r_acc, rs_sem.at[f, h, stage, 2], rr_sem.at[f, h, stage, 2], {axis: to})
+
+    def stage_open(f, h, stage):
+        for c in (stage_far(f, h, stage), stage_near(f, h, stage)):
+            c.start()
+            pending.append(c.wait_send)
+
+    def stage_relay(f, h, stage):
+        axis, way, chunk, r_in, r_acc, r_dir, r_out = stage_refs(f, h, stage)
+        stage_far(f, h, stage).wait_recv()
+        r_out[...] = r_in[...] + chunk(ring(axis, way)[0])[...]
+        relay = stage_next(f, h, stage)
         relay.start()
         pending.append(relay.wait_send)
 
-    def stage_close(f, stage):
-        axis, way, chunk, r_in, r_acc, r_dir, r_out = stage_refs(f, stage)
-        far, near, relay = stage_copies(f, stage)
-        near.wait_recv()
-        relay.wait_recv()
+    def stage_close(f, h, stage):
+        axis, way, chunk, r_in, r_acc, r_dir, r_out = stage_refs(f, h, stage)
+        stage_near(f, h, stage).wait_recv()
+        stage_next(f, h, stage).wait_recv()
         return chunk(me[AXES.index(axis)])[...] + r_acc[...] + r_dir[...]
 
     block = (lane % 64) // 16
 
-    def contract(f):
-        operand = wz[...]
-        for g in range(4):
-            cut = slice(256 * g, 256 * g + 256)
+    def contract_z(f, h, slot):
+        zs = []
+        for n in range(4):
+            operand = wz[n]
+            cut = slice(256 * n + 128 * h, 256 * n + 128 * h + 128)
             both = dot(xh[f, cut], operand)
-            z = (both[:, :128] + both[:, 128:]) + dot(xl[f, cut], operand[:, :128])
+            zs.append((both[:, :128] + both[:, 128:]) + dot(xl[f, cut], operand[:, :128]))
+        for g in range(2):
+            for e in range(2):
+                pair = [z[NJ * g : NJ * g + NJ] for z in zs[2 * e : 2 * e + 2]]
+                hi, lo = split(jnp.concatenate(pair, axis=1))
+                zb[slot, g, e] = jnp.concatenate([hi, lo], axis=0)
+
+    def contract_y(f, h, slot):
+        for g in range(2):
             done = []
-            for h in range(2):
-                pair = [z[NJ * n : NJ * n + NJ] for n in (2 * h, 2 * h + 1)]
-                hi, lo = split(jnp.concatenate(pair, axis=1))
-                y = dot(fyt[...], jnp.concatenate([hi, hi, lo], axis=0))
+            for e in range(2):
+                both = zb[slot, g, e]
+                y = dot(fyt[...], jnp.concatenate([both[:NJ], both], axis=0))
                 done += [tiles(y[:, :128]), tiles(y[:, 128:])]
             for r in range(4):
                 out = []
                 for q in range(8):
-                    acc = done[r][q]
-                    for n in range(4):
-                        if n != r:
-                            moved = pltpu.roll(done[n][q], (16 * (n - r)) % 128, 1)
-                            acc = jnp.where(block == n, moved, acc)
+                    acc = done[-r % 4][q]
+                    for b in range(1, 4):
+                        acc = jnp.where(block == b, done[(b - r) % 4][q], acc)
                     out.append(acc)
-                u[f, r, g] = join(out)
-
-    for f in ORDER:
-        if f != 3:
-            fix(f)
-        contract(f)
-        stage_open(f, 0)
-    for f in ORDER:
-        stage_relay(f, 0)
-    for f in ORDER:
-        whole = stage_close(f, 0)
+                u[f, r, 2 * h + g] = join(out)
+
+    steps = [(f, h) for f in ORDER for h in range(2)]
+    contract_z(*steps[0], 0)
+    for n, (f, h) in enumerate(steps):
+        if n + 1 < len(steps):
+            if h == 1:
+                fix(steps[n + 1][0])
+            contract_z(*steps[n + 1], (n + 1) % 2)
+        contract_y(f, h, n % 2)
+        stage_open(f, h, 0)
+    items = [(f, h) for f in ORDER for h in range(2)]
+    for f, h in items:
+        stage_relay(f, h, 0)
+    for f, h in items:
+        whole = stage_close(f, h, 0)
         slot = 0 if ROUTES[f][1] == 1 else 1
         if ROUTES[f][0] == "gz":
-            b_src_z[slot] = whole
+            b_src_z[slot, h] = whole
         else:
-            b_src_y[slot] = whole
-        stage_open(f, 1)
-    for f in ORDER:
-        stage_relay(f, 1)
-    for f in ORDER:
-        whole = stage_close(f, 1)
-        for g in range(4):
-            ysc[16 * f : 16 * f + 16, 128 * g : 128 * g + 128] = whole[g]
+            b_src_y[slot, h] = whole
+        stage_open(f, h, 1)
+    for f, h in items:
+        stage_relay(f, h, 1)
+    for f, h in items:
+        whole = stage_close(f, h, 1)
+        for g in range(2):
+            at = 128 * (2 * h + g)
+            ysc[16 * f : 16 * f + 16, at : at + 128] = whole[g]
 
     hi, lo = split(ysc[...])
-
-    def last_dot(m, _):
+    copies = {}
+    for o in (4, 3, 5, 2, 6, 1, 7, 0):
+        m = lax.rem(me[0] + o, 8)
         v[m] = dot(hi, k_hi[m]) + dot(lo, k_hi[m]) + dot(hi, k_lo[m])
-        return 0
-
-    lax.fori_loop(0, 8, last_dot, 0)
-    copies = [
-        remote(v.at[lax.rem(me[0] + o, 8)], v_recv.at[o - 1], xs_sem.at[o - 1], xr_sem.at[o - 1], line_to[o - 1])
-        for o in range(1, 8)
-    ]
-    for c in copies:
-        c.start()
-        pending.append(c.wait_send)
+        if o:
+            copies[o] = remote(
+                v.at[m], v_recv.at[o - 1], xs_sem.at[o - 1], xr_sem.at[o - 1], line_to[o - 1]
+            )
+            copies[o].start()
+            pending.append(copies[o].wait_send)
     total = v[me[0]]
-    for o in range(1, 8):
-        copies[o - 1].wait_recv()
+    for o in (1, 7, 2, 6, 3, 5, 4):
+        copies[o].wait_recv()
         total = total + v_recv[o - 1]
     for a in range(8):
         moved = total if a == 0 else pltpu.roll(total, 128 - 16 * a, 1)
@@ -733,7 +748,8 @@
         pltpu.VMEM((2, 8, NK), F32),
         pltpu.VMEM((len(PLANE), 8, NK), F32),
         pltpu.VMEM((7, 8, NK), F32),
-        pltpu.VMEM((256, 256), BF16),
+        pltpu.VMEM((4, 256, 256), BF16),
+        pltpu.VMEM((2, 2, 2, 128, 256), BF16),
         pltpu.VMEM((64, 192), BF16),
         pltpu.VMEM((8, 512, 128), BF16),
         pltpu.VMEM((8, 512, 128), BF16),
@@ -741,10 +757,10 @@
         pltpu.VMEM((4, 1024, 256), BF16),
         pltpu.VMEM((4, 4, 4, 64, 128), F32),
     ]
-    scratch += [pltpu.VMEM((2, 4, 64, 128), F32)] * 4
-    scratch += [pltpu.VMEM((2, 4, 4, 16, 128), F32)] * 4
-    scratch += [pltpu.VMEM((2, 4, 64, 128), F32), pltpu.VMEM((2, 4, 4, 16, 128), F32)]
-    scratch += [pltpu.VMEM((4, 4, 16, 128), F32)] * 4
+    scratch += [pltpu.VMEM((2, 2, 2, 64, 128), F32)] * 4
+    scratch += [pltpu.VMEM((2, 2, 4, 2, 16, 128), F32)] * 4
+    scratch += [pltpu.VMEM((2, 2, 2, 64, 128), F32), pltpu.VMEM((2, 2, 4, 2, 16, 128), F32)]
+    scratch += [pltpu.VMEM((4, 2, 2, 16, 128), F32)] * 4
     scratch += [
         pltpu.VMEM((64, 512), F32),
         pltpu.VMEM((8, 64, 128), F32),
@@ -754,8 +770,8 @@
         dma((5, 6, 2)),
         dma((2, len(PLANE))),
         dma((2, len(PLANE))),
-        dma((4, 2, 3)),
-        dma((4, 2, 3)),
+        dma((4, 2, 2, 3)),
+        dma((4, 2, 2, 3)),
         dma((7,)),
         dma((7,)),
     ]

time: 74.1 us -> 70.2 us (0.947)
  Pallas kernels: 69.9 us -> 66.1 us
    pallas_call x1, Pallas kernels: 69.9 us -> 66.1 us  [per_device(): pl.pallas_call(kernel, out_shape=(pltpu.VMEM(inv_density.shape, F32), plt...]
where the time goes in v5:
time: 70.2 us; the launch traced here: 70.1 us
  Pallas kernels  66.1 us (94%)
  local copies, waits for them, and re-layouts  3.34 us (5%)
    pallas_call x1, Pallas kernels, per_device(): pl.pallas_call(kernel, out_shape=(pltpu.VMEM(inv_density.shape, F32), plt...  66.1 us
    unnamed x3, local copies, waits for them, and re-layouts  3.34 us

profile of v5, /device:TPU:1, one launch (start us, length us, event | category | flops | bytes accessed | tf_op | source)
XLA Modules:
  0.0 70.1 jit_solution(6491956477479049001)
XLA Ops:
  0.6 66.1 %shard_map.76 = (f32[32,64,128]{2,1,0:T(8,128)S(1)}, f32[3,32,64,128]{3,2,1,0:T(8,128)S(1)}, f32[8,4,16,16]{3,2,1,0:T(8,128)S(1)}) custom-call(f32[3,32,64,128]{3,2,1,0:T(8,128)} %vel.1, f32[32,64,128]{2,1,0:T(8,128)} %inv.1, f32[32,64]{1,0:T(8,128)} %fx.1, f32[64,64]{1,0:T(8,128)} %fy.1, f32[64,128]{1,0:T(8,128)} %bitcast.1), custom_call_target="tpu_custom_call" | custom-call | tf_op jit(solution)/shard_map/pallas_call | solution.py:778
  66.7 1.0 %copy.11 = f32[32,64,128]{2,1,0:T(8,128)} copy(f32[32,64,128]{2,1,0:T(8,128)S(1)} %get-tuple-element.3) | data formatting | bytes 2097152
  67.7 0.7 %copy.13 = f32[8,4,16,16]{3,2,1,0:T(8,128)} copy(f32[8,4,16,16]{3,2,1,0:T(8,128)S(1)} %get-tuple-element.5) | data formatting | bytes 65536
  68.4 1.7 %copy.12 = f32[3,32,64,128]{3,2,1,0:T(8,128)} copy(f32[3,32,64,128]{3,2,1,0:T(8,128)S(1)} %get-tuple-element.4) | data formatting | bytes 6291456

commit v6 on v5

--- a/solution.py
+++ b/solution.py
@@ -68,7 +68,7 @@
     one = (jnp.ones_like(r), jnp.zeros_like(r))
     two = (jnp.full_like(r, 2.0), jnp.zeros_like(r))
     y = (r, jnp.zeros_like(r))
-    for _ in range(2):
+    for _ in range(1):
         y = df_mul(y, df_add(two, df_neg(df_mul(x, y))))
     return y
 
@@ -128,8 +128,8 @@
     vx, vy, vz, ip, w0, w1, w2, w3, cx, cy, cz, dinv, pp,
     part, xrecv, xrecv0, xcoef, ysend, yrecv, yrecv0, yown, ycoef, yf, yd,
     zsend, zrecv, zsend0, zrecv0,
-    a_send, a_recv0, a_recv1,
-    wz, zb, fyt, k_hi, k_lo, xh, xl, u,
+    zc, zf, mom, a_send, a_recv0, a_recv1,
+    wz, zb, fyt, k_hi, k_lo, xh, xl, u, uk,
     za_in, za_acc, za_dir, za_out, ya_in, ya_acc, ya_dir, ya_out,
     b_src_z, b_src_y, b_in, b_acc, b_dir, b_out, ysc, v, v_recv,
     in_sem, hs_sem, hr_sem, as_sem, ar_sem, rs_sem, rr_sem, xs_sem, xr_sem,
@@ -311,6 +311,10 @@
         s, e = two_sum(acc[0], parts[0])
         return s, acc[1] + e
 
+    def keep_moment(m, acc):
+        mom[m, 0] = acc[0]
+        mom[m, 1] = acc[1]
+
     def mul(a, b):
         return [x * y for x, y in zip(a, b)]
 
@@ -351,7 +355,7 @@
     hn = opposite_faces(zrecv0[1, 1], zrecv0[0, 1])
     hu = opposite_faces(zrecv0[1, 0], zrecv0[0, 0])
     hu = [jnp.where(odd_lane, -a, a) for a in hu]
-    zcoef = [0.5 * (a + b) for a, b in zip(hn, fn)]
+    zc[...] = join([0.5 * (a + b) for a, b in zip(hn, fn)])
     yd[...] = 0.5 * yrecv0[:, 1]
     yf[0] = -yrecv0[0, 0]
     yf[1] = yrecv0[1, 0]
@@ -382,69 +386,7 @@
         return faces, accumulate(acc, terms)
 
     faces, acc = lax.fori_loop(0, NI // GROUP, first, (no_faces, (zero_acc, zero_acc)))
-    moments = [acc]
-
-    for k in range(ITERS):
-        zsend[k] = join(faces)
-        halo_start(k + 1, range(6))
-        last = k == ITERS - 1
-        here = w[k]
-
-        def inner(t, odd):
-            terms = []
-            for g in range(GROUP):
-                i = t * GROUP + g
-                c = here[i + 1, pl.ds(TOP, NJ)]
-                f = cz[i]
-                bw = cx[i] * here[i, pl.ds(TOP, NJ)] + cx[i + 1] * here[i + 2, pl.ds(TOP, NJ)]
-                bw = bw + cy[i, pl.ds(TOP - 1, NJ)] * here[i + 1, pl.ds(TOP - 1, NJ)]
-                bw = bw + cy[i, pl.ds(TOP, NJ)] * here[i + 1, pl.ds(TOP + 1, NJ)]
-                nxt = join([pltpu.roll(a, NK - 1, 1) for a in tiles(c)])
-                prv = join([pltpu.roll(a, 1, 1) for a in tiles(f * c)])
-                bw = bw + (f * nxt + prv)
-                part[i] = bw
-                terms += tiles(c * bw)
-            return accumulate(odd, terms)
-
-        odd = lax.fori_loop(0, NI // GROUP, inner, (zero_acc, zero_acc))
-
-        halo_wait(k + 1, range(6))
-        flux = mul(zcoef, opposite_faces(zrecv[k, 1], zrecv[k, 0]))
-        terms = mul(flux, faces)
-        for s in range(2):
-            side = ycoef[s] * yrecv[k, s]
-            yf[s] = side
-            terms += tiles(side * ysend[k, s])
-            side = xcoef[s] * xrecv[k, s]
-            edge = (0, NI - 1)[s]
-            terms += tiles(side * here[edge + 1, pl.ds(TOP, NJ)])
-            if not last:
-                part[edge] = part[edge] + side
-        while len(terms) & (len(terms) - 1):
-            terms.append(zero_acc)
-        moments.append(accumulate(odd, terms))
-        if last:
-            break
-        there = w[k + 1]
-
-        def outer(t, carry):
-            faces, even = carry
-            terms = []
-            for g in range(GROUP):
-                i = t * GROUP + g
-                row = pl.ds(i, 1)
-                bw = add_rows(tiles(part[i]), yf, i)
-                bw = [a + b for a, b in zip(bw, at_ends(flux, i))]
-                new = mul(bw, tiles(dinv[i]))
-                there[i + 1, pl.ds(TOP, NJ)] = join(new)
-                ysend[k + 1, 0, row] = new[0][0:1]
-                ysend[k + 1, 1, row] = new[7][7:8]
-                faces = pack(faces, new, i)
-                terms += mul(bw, new)
-            return faces, accumulate(even, terms)
-
-        faces, even = lax.fori_loop(0, NI // GROUP, outer, (no_faces, (zero_acc, zero_acc)))
-        moments.append(even)
+    keep_moment(0, acc)
 
     def build_operands():
         twice = jnp.concatenate([fz[...], fz[...]], axis=0).T
@@ -473,12 +415,131 @@
 
         lax.fori_loop(0, 8, build_x, 0)
 
+    def keep(f, i, x, odd_plane):
+        hi, lo = split(x)
+        rr = pl.ds(pl.multiple_of((lax.rem(i // 2, 4) * 4 + i // 8) * NJ, NJ), NJ)
+        cc = slice(NK * odd_plane, NK * odd_plane + NK)
+        xh[f, rr, cc] = hi
+        xl[f, rr, cc] = lo
+
+    block = (lane % 64) // 16
+
+    def contract_z(f, h, slot):
+        zs = []
+        for n in range(4):
+            operand = wz[n]
+            cut = slice(256 * n + 128 * h, 256 * n + 128 * h + 128)
+            both = dot(xh[f, cut], operand)
+            zs.append((both[:, :128] + both[:, 128:]) + dot(xl[f, cut], operand[:, :128]))
+        for g in range(2):
+            for e in range(2):
+                pair = [z[NJ * g : NJ * g + NJ] for z in zs[2 * e : 2 * e + 2]]
+                hi, lo = split(jnp.concatenate(pair, axis=1))
+                zb[slot, g, e] = jnp.concatenate([hi, lo], axis=0)
+
+    def contract_y(h, slot, dst):
+        for g in range(2):
+            done = []
+            for e in range(2):
+                both = zb[slot, g, e]
+                y = dot(fyt[...], jnp.concatenate([both[:NJ], both], axis=0))
+                done += [tiles(y[:, :128]), tiles(y[:, 128:])]
+            for r in range(4):
+                out = []
+                for q in range(8):
+                    acc = done[-r % 4][q]
+                    for b in range(1, 4):
+                        acc = jnp.where(block == b, done[(b - r) % 4][q], acc)
+                    out.append(acc)
+                dst[r, 2 * h + g] = join(out)
+
+    def contract_vector(k):
+        def body(t, _):
+            for g in range(GROUP):
+                i = t * GROUP + g
+                keep(3, i, w[k][i + 1, pl.ds(TOP, NJ)], g % 2)
+            return 0
+
+        lax.fori_loop(0, NI // GROUP, body, 0)
+        for h in range(2):
+            contract_z(3, h, h)
+        for h in range(2):
+            contract_y(h, h, uk.at[k])
+
+    for k in range(ITERS):
+        zsend[k] = join(faces)
+        halo_start(k + 1, range(6))
+        last = k == ITERS - 1
+        here = w[k]
+
+        def inner(t, odd):
+            terms = []
+            for g in range(GROUP):
+                i = t * GROUP + g
+                c = here[i + 1, pl.ds(TOP, NJ)]
+                f = cz[i]
+                bw = cx[i] * here[i, pl.ds(TOP, NJ)] + cx[i + 1] * here[i + 2, pl.ds(TOP, NJ)]
+                bw = bw + cy[i, pl.ds(TOP - 1, NJ)] * here[i + 1, pl.ds(TOP - 1, NJ)]
+                bw = bw + cy[i, pl.ds(TOP, NJ)] * here[i + 1, pl.ds(TOP + 1, NJ)]
+                nxt = join([pltpu.roll(a, NK - 1, 1) for a in tiles(c)])
+                prv = join([pltpu.roll(a, 1, 1) for a in tiles(f * c)])
+                bw = bw + (f * nxt + prv)
+                part[i] = bw
+                terms += tiles(c * bw)
+            return accumulate(odd, terms)
+
+        keep_moment(2 * k + 1, lax.fori_loop(0, NI // GROUP, inner, (zero_acc, zero_acc)))
+
+        if k == 0:
+            build_operands()
+        else:
+            contract_vector(k - 1)
+
+        halo_wait(k + 1, range(6))
+        flux = mul(tiles(zc[...]), opposite_faces(zrecv[k, 1], zrecv[k, 0]))
+        terms = mul(flux, tiles(zsend[k]))
+        zf[...] = join(flux)
+        for s in range(2):
+            side = ycoef[s] * yrecv[k, s]
+            yf[s] = side
+            terms += tiles(side * ysend[k, s])
+            side = xcoef[s] * xrecv[k, s]
+            edge = (0, NI - 1)[s]
+            terms += tiles(side * here[edge + 1, pl.ds(TOP, NJ)])
+            if not last:
+                part[edge] = part[edge] + side
+        while len(terms) & (len(terms) - 1):
+            terms.append(zero_acc)
+        keep_moment(2 * k + 1, accumulate((mom[2 * k + 1, 0], mom[2 * k + 1, 1]), terms))
+        if last:
+            break
+        there = w[k + 1]
+
+        def outer(t, carry):
+            faces, even = carry
+            terms = []
+            for g in range(GROUP):
+                i = t * GROUP + g
+                row = pl.ds(i, 1)
+                bw = add_rows(tiles(part[i]), yf, i)
+                bw = [a + b for a, b in zip(bw, at_ends(tiles(zf[...]), i))]
+                new = mul(bw, tiles(dinv[i]))
+                there[i + 1, pl.ds(TOP, NJ)] = join(new)
+                ysend[k + 1, 0, row] = new[0][0:1]
+                ysend[k + 1, 1, row] = new[7][7:8]
+                faces = pack(faces, new, i)
+                terms += mul(bw, new)
+            return faces, accumulate(even, terms)
+
+        faces, even = lax.fori_loop(0, NI // GROUP, outer, (no_faces, (zero_acc, zero_acc)))
+        keep_moment(2 * k + 2, even)
+
     row8 = rows((8, NK))
     lane8 = lanes((8, NK))
     hi = zero_acc
     lo = zero_acc
-    for m, acc in enumerate(moments):
-        acc = exact_sum(acc)
+    for m in range(2 * ITERS):
+        acc = exact_sum((mom[m, 0], mom[m, 1]))
         hi = jnp.where(row8 == m, acc[0], hi)
         lo = jnp.where(row8 == m, acc[1], lo)
     total = (hi, lo)
@@ -494,7 +555,7 @@
         for c in copies:
             c.start()
         if stage == 0:
-            build_operands()
+            contract_vector(ITERS - 1)
         for c in copies:
             c.wait_recv()
         terms = [total]
@@ -519,19 +580,78 @@
             total = total + c * x
         return total
 
+    def ring(axis, way):
+        a = AXES.index(axis)
+        n = SIZES[a]
+        to = lax.rem(me[a] + (n + way), n)
+        back = lax.rem(me[a] + (n - way), n)
+        opposite = lax.rem(me[a] + 2, n)
+        return to, back, opposite
+
+    def rows16(m):
+        return pl.ds(pl.multiple_of(m * 16, 16), 16)
+
+    def stage_refs(f, h, stage):
+        axis, way = ROUTES[f]
+        slot = 0 if way == 1 else 1
+        part_ = pl.ds(2 * h, 2)
+        if stage == 0:
+            if axis == "gz":
+                return axis, way, (lambda m: u.at[f, m, part_]), za_in.at[slot, h], za_acc.at[slot, h], za_dir.at[slot, h], za_out.at[slot, h]
+            return axis, way, (lambda m: u.at[f, :, part_, rows16(m)]), ya_in.at[slot, h], ya_acc.at[slot, h], ya_dir.at[slot, h], ya_out.at[slot, h]
+        other = "gy" if axis == "gz" else "gz"
+        if axis == "gz":
+            chunk = lambda m: b_src_z.at[slot, h, :, rows16(m)]
+        else:
+            chunk = lambda m: b_src_y.at[slot, h, m]
+        return other, way, chunk, b_in.at[f, h], b_acc.at[f, h], b_dir.at[f, h], b_out.at[f, h]
+
+    def stage_far(f, h, stage):
+        axis, way, chunk, r_in, r_acc, r_dir, r_out = stage_refs(f, h, stage)
+        to, back, opposite = ring(axis, way)
+        return remote(chunk(opposite), r_in, rs_sem.at[f, h, stage, 0], rr_sem.at[f, h, stage, 0], {axis: to})
+
+    def stage_near(f, h, stage):
+        axis, way, chunk, r_in, r_acc, r_dir, r_out = stage_refs(f, h, stage)
+        to, back, opposite = ring(axis, way)
+        return remote(chunk(back), r_dir, rs_sem.at[f, h, stage, 1], rr_sem.at[f, h, stage, 1], {axis: back})
+
+    def stage_next(f, h, stage):
+        axis, way, chunk, r_in, r_acc, r_dir, r_out = stage_refs(f, h, stage)
+        to, back, opposite = ring(axis, way)
+        return remote(r_out, r_acc, rs_sem.at[f, h, stage, 2], rr_sem.at[f, h, stage, 2], {axis: to})
+
+    def stage_open(f, h, stage):
+        for c in (stage_far(f, h, stage), stage_near(f, h, stage)):
+            c.start()
+            pending.append(c.wait_send)
+
+    def stage_relay(f, h, stage):
+        axis, way, chunk, r_in, r_acc, r_dir, r_out = stage_refs(f, h, stage)
+        stage_far(f, h, stage).wait_recv()
+        r_out[...] = r_in[...] + chunk(ring(axis, way)[0])[...]
+        relay = stage_next(f, h, stage)
+        relay.start()
+        pending.append(relay.wait_send)
+
+    def stage_close(f, h, stage):
+        axis, way, chunk, r_in, r_acc, r_dir, r_out = stage_refs(f, h, stage)
+        stage_near(f, h, stage).wait_recv()
+        stage_next(f, h, stage).wait_recv()
+        return chunk(me[AXES.index(axis)])[...] + r_acc[...] + r_dir[...]
+
+    for h in range(2):
+        for g in range(2 * h, 2 * h + 2):
+            for r in range(4):
+                u[3, r, g] = combine([uk[k, r, g] for k in range(ITERS)])
+        stage_open(3, h, 0)
+
     pe = [opposite_faces(zrecv[k, 1], zrecv[k, 0]) for k in range(ITERS)]
     pe = [combine(list(parts)) for parts in zip(*pe)]
     pe = [jnp.where(odd_lane, -a, a) for a in pe]
     for s in range(2):
         pp[(0, NI + 1)[s], pl.ds(TOP, NJ)] = combine([xrecv[k, s] for k in range(ITERS)])
         yf[s] = combine([yrecv[k, s] for k in range(ITERS)])
-
-    def keep(f, i, x, odd_plane):
-        hi, lo = split(x)
-        rr = pl.ds(pl.multiple_of((lax.rem(i // 2, 4) * 4 + i // 8) * NJ, NJ), NJ)
-        cc = slice(NK * odd_plane, NK * odd_plane + NK)
-        xh[f, rr, cc] = hi
-        xl[f, rr, cc] = lo
 
     def press(t, _):
         for g in range(GROUP):
@@ -541,7 +661,6 @@
             x = combine([ref[i + 1, pl.ds(TOP, NJ)] for ref in w])
             pp[i + 1, pl.ds(TOP, NJ)] = x
             pst[i] = x
-            keep(3, i, x, g % 2)
         return 0
 
     lax.fori_loop(0, NI // GROUP, press, 0)
@@ -568,105 +687,15 @@
 
         lax.fori_loop(0, NI // GROUP, body, 0)
 
-    def ring(axis, way):
-        a = AXES.index(axis)
-        n = SIZES[a]
-        to = lax.rem(me[a] + (n + way), n)
-        back = lax.rem(me[a] + (n - way), n)
-        opposite = lax.rem(me[a] + 2, n)
-        return to, back, opposite
-
-    def rows16(m):
-        return pl.ds(pl.multiple_of(m * 16, 16), 16)
-
-    def stage_refs(f, h, stage):
-        axis, way = ROUTES[f]
-        slot = 0 if way == 1 else 1
-        part_ = pl.ds(2 * h, 2)
-        if stage == 0:
-            if axis == "gz":
-                return axis, way, (lambda m: u.at[f, m, part_]), za_in.at[slot, h], za_acc.at[slot, h], za_dir.at[slot, h], za_out.at[slot, h]
-            return axis, way, (lambda m: u.at[f, :, part_, rows16(m)]), ya_in.at[slot, h], ya_acc.at[slot, h], ya_dir.at[slot, h], ya_out.at[slot, h]
-        other = "gy" if axis == "gz" else "gz"
-        if axis == "gz":
-            chunk = lambda m: b_src_z.at[slot, h, :, rows16(m)]
-        else:
-            chunk = lambda m: b_src_y.at[slot, h, m]
-        return other, way, chunk, b_in.at[f, h], b_acc.at[f, h], b_dir.at[f, h], b_out.at[f, h]
-
-    def stage_far(f, h, stage):
-        axis, way, chunk, r_in, r_acc, r_dir, r_out = stage_refs(f, h, stage)
-        to, back, opposite = ring(axis, way)
-        return remote(chunk(opposite), r_in, rs_sem.at[f, h, stage, 0], rr_sem.at[f, h, stage, 0], {axis: to})
-
-    def stage_near(f, h, stage):
-        axis, way, chunk, r_in, r_acc, r_dir, r_out = stage_refs(f, h, stage)
-        to, back, opposite = ring(axis, way)
-        return remote(chunk(back), r_dir, rs_sem.at[f, h, stage, 1], rr_sem.at[f, h, stage, 1], {axis: back})
-
-    def stage_next(f, h, stage):
-        axis, way, chunk, r_in, r_acc, r_dir, r_out = stage_refs(f, h, stage)
-        to, back, opposite = ring(axis, way)
-        return remote(r_out, r_acc, rs_sem.at[f, h, stage, 2], rr_sem.at[f, h, stage, 2], {axis: to})
-
-    def stage_open(f, h, stage):
-        for c in (stage_far(f, h, stage), stage_near(f, h, stage)):
-            c.start()
-            pending.append(c.wait_send)
-
-    def stage_relay(f, h, stage):
-        axis, way, chunk, r_in, r_acc, r_dir, r_out = stage_refs(f, h, stage)
-        stage_far(f, h, stage).wait_recv()
-        r_out[...] = r_in[...] + chunk(ring(axis, way)[0])[...]
-        relay = stage_next(f, h, stage)
-        relay.start()
-        pending.append(relay.wait_send)
-
-    def stage_close(f, h, stage):
-        axis, way, chunk, r_in, r_acc, r_dir, r_out = stage_refs(f, h, stage)
-        stage_near(f, h, stage).wait_recv()
-        stage_next(f, h, stage).wait_recv()
-        return chunk(me[AXES.index(axis)])[...] + r_acc[...] + r_dir[...]
-
-    block = (lane % 64) // 16
-
-    def contract_z(f, h, slot):
-        zs = []
-        for n in range(4):
-            operand = wz[n]
-            cut = slice(256 * n + 128 * h, 256 * n + 128 * h + 128)
-            both = dot(xh[f, cut], operand)
-            zs.append((both[:, :128] + both[:, 128:]) + dot(xl[f, cut], operand[:, :128]))
-        for g in range(2):
-            for e in range(2):
-                pair = [z[NJ * g : NJ * g + NJ] for z in zs[2 * e : 2 * e + 2]]
-                hi, lo = split(jnp.concatenate(pair, axis=1))
-                zb[slot, g, e] = jnp.concatenate([hi, lo], axis=0)
-
-    def contract_y(f, h, slot):
-        for g in range(2):
-            done = []
-            for e in range(2):
-                both = zb[slot, g, e]
-                y = dot(fyt[...], jnp.concatenate([both[:NJ], both], axis=0))
-                done += [tiles(y[:, :128]), tiles(y[:, 128:])]
-            for r in range(4):
-                out = []
-                for q in range(8):
-                    acc = done[-r % 4][q]
-                    for b in range(1, 4):
-                        acc = jnp.where(block == b, done[(b - r) % 4][q], acc)
-                    out.append(acc)
-                u[f, r, 2 * h + g] = join(out)
-
-    steps = [(f, h) for f in ORDER for h in range(2)]
+    steps = [(f, h) for f in ORDER[1:] for h in range(2)]
+    fix(ORDER[1])
     contract_z(*steps[0], 0)
     for n, (f, h) in enumerate(steps):
         if n + 1 < len(steps):
             if h == 1:
                 fix(steps[n + 1][0])
             contract_z(*steps[n + 1], (n + 1) % 2)
-        contract_y(f, h, n % 2)
+        contract_y(h, n % 2, u.at[f])
         stage_open(f, h, 0)
     items = [(f, h) for f in ORDER for h in range(2)]
     for f, h in items:
@@ -745,6 +774,9 @@
         pltpu.VMEM((ITERS, 2, 32, NK), F32),
         pltpu.VMEM((2, 32, NK), F32),
         pltpu.VMEM((2, 2, 32, NK), F32),
+        pltpu.VMEM((32, NK), F32),
+        pltpu.VMEM((32, NK), F32),
+        pltpu.VMEM((8, 2, 8, NK), F32),
         pltpu.VMEM((2, 8, NK), F32),
         pltpu.VMEM((len(PLANE), 8, NK), F32),
         pltpu.VMEM((7, 8, NK), F32),
@@ -756,6 +788,7 @@
         pltpu.VMEM((4, 1024, 256), BF16),
         pltpu.VMEM((4, 1024, 256), BF16),
         pltpu.VMEM((4, 4, 4, 64, 128), F32),
+        pltpu.VMEM((ITERS, 4, 4, 64, 128), F32),
     ]
     scratch += [pltpu.VMEM((2, 2, 2, 64, 128), F32)] * 4
     scratch += [pltpu.VMEM((2, 2, 4, 2, 16, 128), F32)] * 4

time: 70.2 us -> 71 us (1.011)
  Pallas kernels: 66.1 us -> 66.9 us
    pallas_call x1, Pallas kernels: 66.1 us -> 66.9 us  [per_device(): pl.pallas_call(kernel, out_shape=(pltpu.VMEM(inv_density.shape, F32), plt...]
where the time goes in v6:
time: 71 us; the launch traced here: 70.8 us
  Pallas kernels  66.9 us (94%)
  local copies, waits for them, and re-layouts  3.34 us (5%)
    pallas_call x1, Pallas kernels, per_device(): pl.pallas_call(kernel, out_shape=(pltpu.VMEM(inv_density.shape, F32), plt...  66.9 us
    unnamed x3, local copies, waits for them, and re-layouts  3.34 us

profile of v6, /device:TPU:1, one launch (start us, length us, event | category | flops | bytes accessed | tf_op | source)
XLA Modules:
  0.0 70.8 jit_solution(17912573206812439163)
XLA Ops:
  0.6 66.9 %shard_map.76 = (f32[32,64,128]{2,1,0:T(8,128)S(1)}, f32[3,32,64,128]{3,2,1,0:T(8,128)S(1)}, f32[8,4,16,16]{3,2,1,0:T(8,128)S(1)}) custom-call(f32[3,32,64,128]{3,2,1,0:T(8,128)} %vel.1, f32[32,64,128]{2,1,0:T(8,128)} %inv.1, f32[32,64]{1,0:T(8,128)} %fx.1, f32[64,64]{1,0:T(8,128)} %fy.1, f32[64,128]{1,0:T(8,128)} %bitcast.1), custom_call_target="tpu_custom_call" | custom-call | tf_op jit(solution)/shard_map/pallas_call | solution.py:811
  67.5 1.0 %copy.11 = f32[32,64,128]{2,1,0:T(8,128)} copy(f32[32,64,128]{2,1,0:T(8,128)S(1)} %get-tuple-element.3) | data formatting | bytes 2097152
  68.5 0.7 copy.13
  69.2 1.7 %copy.12 = f32[3,32,64,128]{3,2,1,0:T(8,128)} copy(f32[3,32,64,128]{3,2,1,0:T(8,128)S(1)} %get-tuple-element.4) | data formatting | bytes 6291456

commit v7 on v6

--- a/solution.py
+++ b/solution.py
@@ -399,6 +399,8 @@
         fyp = jnp.concatenate([fy[...], jnp.zeros((NJ, 64), F32)], axis=1)
         hi, lo = split(fyp.T[:64])
         fyt[...] = jnp.concatenate([hi, lo, hi], axis=1)
+
+    def build_x_operand():
         fx_hi, fx_lo = split(fx[...])
         row = rows((512, NI))
         pair = ((row % 64) // 16 + 4 - me[2]) % 4
@@ -472,6 +474,11 @@
         last = k == ITERS - 1
         here = w[k]
 
+        if k == 0:
+            build_operands()
+        else:
+            contract_vector(k - 1)
+
         def inner(t, odd):
             terms = []
             for g in range(GROUP):
@@ -489,11 +496,6 @@
             return accumulate(odd, terms)
 
         keep_moment(2 * k + 1, lax.fori_loop(0, NI // GROUP, inner, (zero_acc, zero_acc)))
-
-        if k == 0:
-            build_operands()
-        else:
-            contract_vector(k - 1)
 
         halo_wait(k + 1, range(6))
         flux = mul(tiles(zc[...]), opposite_faces(zrecv[k, 1], zrecv[k, 0]))
@@ -556,6 +558,8 @@
             c.start()
         if stage == 0:
             contract_vector(ITERS - 1)
+        else:
+            build_x_operand()
         for c in copies:
             c.wait_recv()
         terms = [total]

time: 71 us -> 69.8 us (0.983)
  Pallas kernels: 66.9 us -> 65.6 us
    pallas_call x1, Pallas kernels: 66.9 us -> 65.6 us  [per_device(): pl.pallas_call(kernel, out_shape=(pltpu.VMEM(inv_density.shape, F32), plt...]
where the time goes in v7:
time: 69.8 us; the launch traced here: 69.6 us
  Pallas kernels  65.6 us (94%)
  local copies, waits for them, and re-layouts  3.34 us (5%)
    pallas_call x1, Pallas kernels, per_device(): pl.pallas_call(kernel, out_shape=(pltpu.VMEM(inv_density.shape, F32), plt...  65.6 us
    unnamed x3, local copies, waits for them, and re-layouts  3.34 us

profile of v7, /device:TPU:1, one launch (start us, length us, event | category | flops | bytes accessed | tf_op | source)
XLA Modules:
  0.0 69.6 jit_solution(6975364425253500097)
XLA Ops:
  0.6 65.6 %shard_map.76 = (f32[32,64,128]{2,1,0:T(8,128)S(1)}, f32[3,32,64,128]{3,2,1,0:T(8,128)S(1)}, f32[8,4,16,16]{3,2,1,0:T(8,128)S(1)}) custom-call(f32[3,32,64,128]{3,2,1,0:T(8,128)} %vel.1, f32[32,64,128]{2,1,0:T(8,128)} %inv.1, f32[32,64]{1,0:T(8,128)} %fx.1, f32[64,64]{1,0:T(8,128)} %fy.1, f32[64,128]{1,0:T(8,128)} %bitcast.1), custom_call_target="tpu_custom_call" | custom-call | tf_op jit(solution)/shard_map/pallas_call | solution.py:815
  66.2 1.0 %copy.11 = f32[32,64,128]{2,1,0:T(8,128)} copy(f32[32,64,128]{2,1,0:T(8,128)S(1)} %get-tuple-element.3) | data formatting | bytes 2097152
  67.2 0.7 %copy.13 = f32[8,4,16,16]{3,2,1,0:T(8,128)} copy(f32[8,4,16,16]{3,2,1,0:T(8,128)S(1)} %get-tuple-element.5) | data formatting | bytes 65536
  67.9 1.7 %copy.12 = f32[3,32,64,128]{3,2,1,0:T(8,128)} copy(f32[3,32,64,128]{3,2,1,0:T(8,128)S(1)} %get-tuple-element.4) | data formatting | bytes 6291456

commit v8 on v7

--- a/solution.py
+++ b/solution.py
@@ -15,7 +15,9 @@
 AXES = ("gx", "gy", "gz")
 SIZES = (8, 4, 4)
 PLANE = [(dy, dz) for dy in range(4) for dz in range(4) if dy or dz]
-ROUTES = {3: ("gz", 1), 1: ("gy", 1), 0: ("gz", -1), 2: ("gy", -1)}
+ROUTES = {
+    (f, h): (("gz", "gy")[h], way) for f, way in ((3, 1), (1, -1), (0, 1), (2, -1)) for h in range(2)
+}
 ORDER = (3, 1, 0, 2)
 TINY = 1e-11
 
@@ -596,18 +598,17 @@
         return pl.ds(pl.multiple_of(m * 16, 16), 16)
 
     def stage_refs(f, h, stage):
-        axis, way = ROUTES[f]
-        slot = 0 if way == 1 else 1
+        axis, way = ROUTES[f, h]
         part_ = pl.ds(2 * h, 2)
         if stage == 0:
             if axis == "gz":
-                return axis, way, (lambda m: u.at[f, m, part_]), za_in.at[slot, h], za_acc.at[slot, h], za_dir.at[slot, h], za_out.at[slot, h]
-            return axis, way, (lambda m: u.at[f, :, part_, rows16(m)]), ya_in.at[slot, h], ya_acc.at[slot, h], ya_dir.at[slot, h], ya_out.at[slot, h]
+                return axis, way, (lambda m: u.at[f, m, part_]), za_in.at[f], za_acc.at[f], za_dir.at[f], za_out.at[f]
+            return axis, way, (lambda m: u.at[f, :, part_, rows16(m)]), ya_in.at[f], ya_acc.at[f], ya_dir.at[f], ya_out.at[f]
         other = "gy" if axis == "gz" else "gz"
         if axis == "gz":
-            chunk = lambda m: b_src_z.at[slot, h, :, rows16(m)]
+            chunk = lambda m: b_src_z.at[f, :, rows16(m)]
         else:
-            chunk = lambda m: b_src_y.at[slot, h, m]
+            chunk = lambda m: b_src_y.at[f, m]
         return other, way, chunk, b_in.at[f, h], b_acc.at[f, h], b_dir.at[f, h], b_out.at[f, h]
 
     def stage_far(f, h, stage):
@@ -706,11 +707,10 @@
         stage_relay(f, h, 0)
     for f, h in items:
         whole = stage_close(f, h, 0)
-        slot = 0 if ROUTES[f][1] == 1 else 1
-        if ROUTES[f][0] == "gz":
-            b_src_z[slot, h] = whole
+        if ROUTES[f, h][0] == "gz":
+            b_src_z[f] = whole
         else:
-            b_src_y[slot, h] = whole
+            b_src_y[f] = whole
         stage_open(f, h, 1)
     for f, h in items:
         stage_relay(f, h, 1)
@@ -794,9 +794,9 @@
         pltpu.VMEM((4, 4, 4, 64, 128), F32),
         pltpu.VMEM((ITERS, 4, 4, 64, 128), F32),
     ]
-    scratch += [pltpu.VMEM((2, 2, 2, 64, 128), F32)] * 4
-    scratch += [pltpu.VMEM((2, 2, 4, 2, 16, 128), F32)] * 4
-    scratch += [pltpu.VMEM((2, 2, 2, 64, 128), F32), pltpu.VMEM((2, 2, 4, 2, 16, 128), F32)]
+    scratch += [pltpu.VMEM((4, 2, 64, 128), F32)] * 4
+    scratch += [pltpu.VMEM((4, 4, 2, 16, 128), F32)] * 4
+    scratch += [pltpu.VMEM((4, 2, 64, 128), F32), pltpu.VMEM((4, 4, 2, 16, 128), F32)]
     scratch += [pltpu.VMEM((4, 2, 2, 16, 128), F32)] * 4
     scratch += [
         pltpu.VMEM((64, 512), F32),

time: 69.8 us -> 69.4 us (level)
  no operation moved by 1% of the time
where the time goes in v8:
time: 69.4 us; the launch traced here: 69.3 us
  Pallas kernels  65.3 us (94%)
  local copies, waits for them, and re-layouts  3.34 us (5%)
    pallas_call x1, Pallas kernels, per_device(): pl.pallas_call(kernel, out_shape=(pltpu.VMEM(inv_density.shape, F32), plt...  65.3 us
    unnamed x3, local copies, waits for them, and re-layouts  3.34 us

profile of v8, /device:TPU:1, one launch (start us, length us, event | category | flops | bytes accessed | tf_op | source)
XLA Modules:
  0.0 69.3 jit_solution(11173919610817645904)
XLA Ops:
  0.6 65.3 %shard_map.76 = (f32[32,64,128]{2,1,0:T(8,128)S(1)}, f32[3,32,64,128]{3,2,1,0:T(8,128)S(1)}, f32[8,4,16,16]{3,2,1,0:T(8,128)S(1)}) custom-call(f32[3,32,64,128]{3,2,1,0:T(8,128)} %vel.1, f32[32,64,128]{2,1,0:T(8,128)} %inv.1, f32[32,64]{1,0:T(8,128)} %fx.1, f32[64,64]{1,0:T(8,128)} %fy.1, f32[64,128]{1,0:T(8,128)} %bitcast.1), custom_call_target="tpu_custom_call" | custom-call | tf_op jit(solution)/shard_map/pallas_call | solution.py:815
  65.9 1.0 %copy.11 = f32[32,64,128]{2,1,0:T(8,128)} copy(f32[32,64,128]{2,1,0:T(8,128)S(1)} %get-tuple-element.3) | data formatting | bytes 2097152
  66.9 0.7 %copy.13 = f32[8,4,16,16]{3,2,1,0:T(8,128)} copy(f32[8,4,16,16]{3,2,1,0:T(8,128)S(1)} %get-tuple-element.5) | data formatting | bytes 65536
  67.6 1.7 %copy.12 = f32[3,32,64,128]{3,2,1,0:T(8,128)} copy(f32[3,32,64,128]{3,2,1,0:T(8,128)S(1)} %get-tuple-element.4) | data formatting | bytes 6291456

commit v9 on v8

--- a/solution.py
+++ b/solution.py
@@ -702,8 +702,11 @@
             contract_z(*steps[n + 1], (n + 1) % 2)
         contract_y(h, n % 2, u.at[f])
         stage_open(f, h, 0)
+        if n == 4:
+            for early in range(2):
+                stage_relay(ORDER[0], early, 0)
     items = [(f, h) for f in ORDER for h in range(2)]
-    for f, h in items:
+    for f, h in steps:
         stage_relay(f, h, 0)
     for f, h in items:
         whole = stage_close(f, h, 0)

time: 69.4 us -> 69.3 us (level)
  no operation moved by 1% of the time
where the time goes in v9:
time: 69.3 us; the launch traced here: 69.2 us
  Pallas kernels  65.2 us (94%)
  local copies, waits for them, and re-layouts  3.34 us (5%)
    pallas_call x1, Pallas kernels, per_device(): pl.pallas_call(kernel, out_shape=(pltpu.VMEM(inv_density.shape, F32), plt...  65.2 us
    unnamed x3, local copies, waits for them, and re-layouts  3.34 us

profile of v9, /device:TPU:1, one launch (start us, length us, event | category | flops | bytes accessed | tf_op | source)
XLA Modules:
  0.0 69.2 jit_solution(4872713559793384505)
XLA Ops:
  0.6 65.2 %shard_map.76 = (f32[32,64,128]{2,1,0:T(8,128)S(1)}, f32[3,32,64,128]{3,2,1,0:T(8,128)S(1)}, f32[8,4,16,16]{3,2,1,0:T(8,128)S(1)}) custom-call(f32[3,32,64,128]{3,2,1,0:T(8,128)} %vel.1, f32[32,64,128]{2,1,0:T(8,128)} %inv.1, f32[32,64]{1,0:T(8,128)} %fx.1, f32[64,64]{1,0:T(8,128)} %fy.1, f32[64,128]{1,0:T(8,128)} %bitcast.1), custom_call_target="tpu_custom_call" | custom-call | tf_op jit(solution)/shard_map/pallas_call | solution.py:818
  65.8 1.0 %copy.11 = f32[32,64,128]{2,1,0:T(8,128)} copy(f32[32,64,128]{2,1,0:T(8,128)S(1)} %get-tuple-element.3) | data formatting | bytes 2097152
  66.8 0.7 %copy.13 = f32[8,4,16,16]{3,2,1,0:T(8,128)} copy(f32[8,4,16,16]{3,2,1,0:T(8,128)S(1)} %get-tuple-element.5) | data formatting | bytes 65536
  67.5 1.7 %copy.12 = f32[3,32,64,128]{3,2,1,0:T(8,128)} copy(f32[3,32,64,128]{3,2,1,0:T(8,128)S(1)} %get-tuple-element.4) | data formatting | bytes 6291456
